TPU v7x, 32 devices: a whole 2x2x4 slice. The times are simulated.
32 devices in a mesh: wide: 8 (over y, x, core), narrow: 4 (over z).
Axes of the slice: x: 2, y: 2, z: 4, core: 2. Of those that a mesh axis runs over, the one named last changes fastest.
Arguments:
- divergence: float32 [64, 32, 512], P('wide', None, 'narrow'), may hold values from -6 to 6
- pressure_start: float32 [64, 32, 512], P('wide', None, 'narrow'), may hold values from -3 to 3
- phase: int32 [64, 32, 512], P('wide', None, 'narrow'), may hold values 0 or 1
- velocity_cot: float32 [3, 64, 32, 512], P(None, 'wide', None, 'narrow'), may hold values from -6 to 6
Outputs:
- grad_divergence: float32 [64, 32, 512], P('wide', None, 'narrow')
- grad_pressure: float32 [64, 32, 512], P('wide', None, 'narrow')
- grad_faces: float32 [3, 64, 32, 512], P(None, 'wide', None, 'narrow')
Inputs may be any that keep to these rules, and one draw needn't show every extreme that they name: `phase`: 0 marks a liquid cell, 1 a gas cell.
All inputs are finite; a program needn't handle non-finite values. No bound on the sum of `phase` on one device may be relied on, other than what follows from the above.
Results may differ from a plain program's by a relative error of at most 0.0003.
Values sent between devices are 32-bit elements; how exact they have to be, the bound alone decides.
No kernel may reach another device: no remote copies, remote signals or barrier semaphores. Data moves between devices by JAX's collectives and lax.ppermute only.
A program may use at most 64 MiB of HBM per device.

v0:
```python
import math

import jax
import jax.numpy as jnp
from jax import lax
from jax.sharding import PartitionSpec as P

SWEEPS = 6


gas_density = 0.25
lower_bound = 0.25
upper_bound = 2.0


def extended_2(shard, sides, width):
    for axis, dim in sides:
        size, length = (lax.axis_size(axis), shard.shape[dim])
        up = [(i, (i + 1) % size) for i in range(size - 1)]
        down = [(j, i) for i, j in up]
        last = lax.slice_in_dim(shard, length - width, length, axis=dim)
        initial = lax.slice_in_dim(shard, 0, width, axis=dim)
        before = lax.ppermute(last, axis, up)
        after = lax.ppermute(initial, axis, down)
        shard = jnp.concatenate([before, shard, after], axis=dim)
    return shard


def passed_along(value, axis, steps):
    count = lax.axis_size(axis)
    initial, last = (max(0, -steps), min(count, count - steps))
    return lax.ppermute(value, axis, [(source, source + steps) for source in range(initial, last)])


def chebyshev_weights(count):
    center = 0.5 * (upper_bound + lower_bound)
    radius = 0.5 * (upper_bound - lower_bound)
    roots = [
        center + radius * math.cos(math.pi * (2 * number + 1) / (2 * count))
        for number in range(count)
    ]
    order = []
    for number in range(count // 2):
        order.append(number)
        order.append(count - 1 - number)
    return [1.0 / roots[position] for position in order]


def shift_up(array, axis_dim):
    length = array.shape[axis_dim]
    zeros = jnp.zeros_like(lax.slice_in_dim(array, 0, 1, axis=axis_dim))
    return jnp.concatenate(
        [lax.slice_in_dim(array, 1, length, axis=axis_dim), zeros], axis=axis_dim
    )


def shift_down(array, axis_dim):
    length = array.shape[axis_dim]
    zeros = jnp.zeros_like(lax.slice_in_dim(array, 0, 1, axis=axis_dim))
    return jnp.concatenate(
        [zeros, lax.slice_in_dim(array, 0, length - 1, axis=axis_dim)], axis=axis_dim
    )


def trim(array, width):
    return array[width : array.shape[0] - width, :, width : array.shape[2] - width]


def apply_operator(field, upper, lower):
    applied = jnp.zeros_like(field)
    for axis_dim in range(3):
        applied = applied + upper[axis_dim] * (field - shift_up(field, axis_dim))
        applied = applied + lower[axis_dim] * (field - shift_down(field, axis_dim))
    return applied


def per_device(divergence, pressure_start, phase, velocity_cot):
    cells_x = divergence.shape[0]
    cells_z = divergence.shape[2]
    group = 3
    margin = group + 1
    density = jnp.where(phase == 1, gas_density, 1.0).astype(jnp.float32)
    stacked = jnp.stack([density, divergence])
    wider = extended_2(stacked, (("wide", 1), ("narrow", 3)), margin + 1)
    dens_wide = wider[0]
    dens_safe = jnp.where(dens_wide > 0.0, dens_wide, 1.0)
    upper = []
    lower = []
    for axis_dim in range(3):
        above = shift_up(dens_wide, axis_dim)
        below = shift_down(dens_wide, axis_dim)
        upper.append(trim(2.0 / (dens_safe + jnp.where(above > 0.0, above, dens_safe)), 1))
        lower.append(trim(2.0 / (dens_safe + jnp.where(below > 0.0, below, dens_safe)), 1))
    source = trim(wider[1], 1)
    inside = (trim(dens_wide, 1) > 0.0).astype(jnp.float32)
    diag = upper[0] + lower[0] + upper[1] + lower[1] + upper[2] + lower[2]
    diag_safe = jnp.where(inside > 0.0, diag, 1.0)
    weights = chebyshev_weights(SWEEPS)
    groups = SWEEPS // group

    def forward_sweep(field, weight):
        return field + inside * (
            weight * (source - apply_operator(field, upper, lower)) / diag_safe
        )

    pressure = pressure_start
    saved = []
    extended = None
    for group_number in range(groups):
        extended = extended_2(pressure, (("wide", 0), ("narrow", 2)), margin)
        states = [extended]
        for inner in range(group):
            extended = forward_sweep(extended, weights[group_number * group + inner])
            states.append(extended)
        saved.append(states[0])
        pressure = trim(extended, margin)
    grad_faces = []
    fluxes = []
    for axis_dim in range(3):
        rise = trim(shift_up(extended, axis_dim) - extended, margin)
        grad_faces.append(-velocity_cot[axis_dim] * rise)
        fluxes.append(trim(upper[axis_dim], margin) * velocity_cot[axis_dim])
    below_x = passed_along(fluxes[0][cells_x - 1 :], "wide", 1)
    below_z = passed_along(fluxes[2][:, :, cells_z - 1 :], "narrow", 1)
    down_x = jnp.concatenate([below_x, fluxes[0][: cells_x - 1]], axis=0)
    down_z = jnp.concatenate([below_z, fluxes[2][:, :, : cells_z - 1]], axis=2)
    adjoint_int = fluxes[0] - down_x + (fluxes[1] - shift_down(fluxes[1], 1)) + (fluxes[2] - down_z)
    grad_source = jnp.zeros_like(divergence)
    for group_number in reversed(range(groups)):
        states = [saved[group_number]]
        for inner in range(group - 1):
            states.append(forward_sweep(states[-1], weights[group_number * group + inner]))
        adjoint = extended_2(adjoint_int, (("wide", 0), ("narrow", 2)), margin)
        for inner in reversed(range(group)):
            weight = weights[group_number * group + inner]
            state = states[inner]
            scaled = inside * (weight * adjoint / diag_safe)
            residual_ext = source - apply_operator(state, upper, lower)
            ratio = scaled * residual_ext / diag_safe
            adjoint = inside * (adjoint - apply_operator(scaled, upper, lower))
            grad_source = grad_source + trim(scaled, margin)
            for axis_dim in range(3):
                term = (scaled - shift_up(scaled, axis_dim)) * (state - shift_up(state, axis_dim))
                term = term + (ratio + shift_up(ratio, axis_dim))
                grad_faces[axis_dim] = grad_faces[axis_dim] - trim(term, margin)
        adjoint_int = trim(adjoint, margin)
    return (grad_source, adjoint_int, jnp.stack(grad_faces))


def solution(mesh):
    in_specs = (
        P("wide", None, "narrow"),
        P("wide", None, "narrow"),
        P("wide", None, "narrow"),
        P(None, "wide", None, "narrow"),
    )
    out_specs = (
        P("wide", None, "narrow"),
        P("wide", None, "narrow"),
        P(None, "wide", None, "narrow"),
    )
    return jax.shard_map(
        per_device, mesh=mesh, in_specs=in_specs, out_specs=out_specs, check_vma=False
    )
```

profile of v0, /device:TPU:28, one launch (start us, length us, event | category | flops | bytes accessed | tf_op | source)
XLA Modules:
  0.0 139.8 jit_solution(13424760165820292553)
XLA Ops:
  3.5 4.5 %collective-permute-start.15 = (f32[4,32,128]{2,1,0:T(8,128)S(1)}, f32[4,32,128]{2,1,0:T(8,128)S(1)}, u32[]{:S(2)}, u32[]{:S(2)}) collective-permute-start(f32[4,32,128]{2,1,0:T(8,128)S(1)} %get-tuple-element.187), channel_id=1, source_target_pairs={{4,0},{8,4},{12,8},{16,12},{20,16},{24,20},{28,24},{5,1},{9,5},{13... | collective-permute-start | bytes 196616 | tf_op jit(solution)/shard_map/ppermute | solution.py:24
  10.1 2.4 %collective-permute-start.17 = (f32[16,32,4]{2,1,0:T(8,128)S(1)}, f32[16,32,4]{2,1,0:T(8,128)S(1)}, u32[]{:S(2)}, u32[]{:S(2)}) collective-permute-start(f32[16,32,4]{2,1,0:T(8,128)S(1)} %get-tuple-element.184), channel_id=1, source_target_pairs={{1,0},{2,1},{3,2},{5,4},{6,5},{7,6},{9,8},{10,9},{11,10},{13,12},{... | collective-permute-start | bytes 24584 | tf_op jit(solution)/shard_map/ppermute | solution.py:24
  13.8 4.3 %collective-permute-start.1 = (f32[2,5,32,128]{3,2,1,0:T(8,128)S(1)}, f32[2,5,32,128]{3,2,1,0:T(8,128)S(1)}, u32[]{:S(2)}, u32[]{:S(2)}) collective-permute-start(f32[2,5,32,128]{3,2,1,0:T(8,128)S(1)} %get-tuple-element.182), channel_id=1, source_target_pairs={{4,0},{8,4},{12,8},{16,12},{20,16},{24,20},{28,24},{5,1},{9,5},{13... | collective-permute-start | bytes 491528 | tf_op jit(solution)/shard_map/ppermute | solution.py:24
  20.0 3.0 %collective-permute-done.16 = f32[16,32,4]{2,1,0:T(8,128)S(1)} collective-permute-done((f32[16,32,4]{2,1,0:T(8,128)S(1)}, f32[16,32,4]{2,1,0:T(8,128)S(1)}, u32[]{:S(2)}, u32[]{:S(2)}) %collective-permute-start.16) | collective-permute-done | bytes 8224 | tf_op jit(solution)/shard_map/ppermute | solution.py:23
  27.8 4.0 %collective-permute-start.3 = (f32[2,18,32,5]{2,0,3,1:T(2,128)}, f32[2,18,32,5]{2,0,3,1:T(2,128)S(1)}, u32[]{:S(2)}, u32[]{:S(2)}) collective-permute-start(f32[2,18,32,5]{2,0,3,1:T(2,128)} %copy.22), channel_id=1, source_target_pairs={{1,0},{2,1},{3,2},{5,4},{6,5},{7,6},{9,8},{10,9},{11,10},{13,12},{... | collective-permute-start | bytes 69128 | tf_op jit(solution)/shard_map/ppermute | solution.py:24
  34.7 3.9 %collective-permute-done.2 = f32[2,18,32,5]{2,0,3,1:T(2,128)} collective-permute-done((f32[2,18,32,5]{2,0,3,1:T(2,128)S(1)}, f32[2,18,32,5]{2,0,3,1:T(2,128)}, u32[]{:S(2)}, u32[]{:S(2)}) %collective-permute-start.2) | collective-permute-done | bytes 23072 | tf_op jit(solution)/shard_map/ppermute | solution.py:23
  52.8 4.5 %collective-permute-start.19 = (f32[4,32,128]{2,1,0:T(8,128)S(1)}, f32[4,32,128]{2,1,0:T(8,128)S(1)}, u32[]{:S(2)}, u32[]{:S(2)}) collective-permute-start(f32[4,32,128]{2,1,0:T(8,128)S(1)} %get-tuple-element.153), channel_id=1, source_target_pairs={{4,0},{8,4},{12,8},{16,12},{20,16},{24,20},{28,24},{5,1},{9,5},{13... | collective-permute-start | bytes 196616 | tf_op jit(solution)/shard_map/ppermute | solution.py:24
  59.8 4.0 %collective-permute-done.18 = f32[4,32,128]{2,1,0:T(8,128)S(1)} collective-permute-done((f32[4,32,128]{2,1,0:T(8,128)S(1)}, f32[4,32,128]{2,1,0:T(8,128)S(1)}, u32[]{:S(2)}, u32[]{:S(2)}) %collective-permute-start.18) | collective-permute-done | bytes 65568 | tf_op jit(solution)/shard_map/ppermute | solution.py:23
  64.0 4.3 %collective-permute-start.21 = (f32[16,32,4]{2,1,0:T(8,128)S(1)}, f32[16,32,4]{2,1,0:T(8,128)S(1)}, u32[]{:S(2)}, u32[]{:S(2)}) collective-permute-start(f32[16,32,4]{2,1,0:T(8,128)S(1)} %get-tuple-element.180), channel_id=1, source_target_pairs={{1,0},{2,1},{3,2},{5,4},{6,5},{7,6},{9,8},{10,9},{11,10},{13,12},{... | collective-permute-start | bytes 24584 | tf_op jit(solution)/shard_map/ppermute | solution.py:24
  71.5 2.6 %collective-permute-start.6 = (f32[4,32,128]{2,1,0:T(8,128)S(1)}, f32[4,32,128]{2,1,0:T(8,128)S(1)}, u32[]{:S(2)}, u32[]{:S(2)}) collective-permute-start(f32[4,32,128]{2,1,0:T(8,128)S(1)} %get-tuple-element.185), channel_id=1, source_target_pairs={{0,4},{4,8},{8,12},{12,16},{16,20},{20,24},{24,28},{1,5},{5,9},{9,... | collective-permute-start | bytes 196616 | tf_op jit(solution)/shard_map/ppermute | solution.py:23
  74.1 2.4 %collective-permute-done.20 = f32[16,32,4]{2,1,0:T(8,128)S(1)} collective-permute-done((f32[16,32,4]{2,1,0:T(8,128)S(1)}, f32[16,32,4]{2,1,0:T(8,128)S(1)}, u32[]{:S(2)}, u32[]{:S(2)}) %collective-permute-start.20) | collective-permute-done | bytes 8224 | tf_op jit(solution)/shard_map/ppermute | solution.py:23
  81.4 2.3 %collective-permute-start.9 = (f32[16,32,4]{2,1,0:T(8,128)S(1)}, f32[16,32,4]{2,1,0:T(8,128)S(1)}, u32[]{:S(2)}, u32[]{:S(2)}) collective-permute-start(f32[16,32,4]{2,1,0:T(8,128)S(1)} %get-tuple-element.178), channel_id=1, source_target_pairs={{1,0},{2,1},{3,2},{5,4},{6,5},{7,6},{9,8},{10,9},{11,10},{13,12},{... | collective-permute-start | bytes 24584 | tf_op jit(solution)/shard_map/ppermute | solution.py:24
  86.7 2.6 %collective-permute-done.9 = f32[16,32,4]{2,1,0:T(8,128)S(1)} collective-permute-done((f32[16,32,4]{2,1,0:T(8,128)S(1)}, f32[16,32,4]{2,1,0:T(8,128)S(1)}, u32[]{:S(2)}, u32[]{:S(2)}) %collective-permute-start.9) | collective-permute-done | bytes 8224 | tf_op jit(solution)/shard_map/ppermute | solution.py:24
  89.3 4.1 %collective-permute-done.8 = f32[16,32,4]{2,1,0:T(8,128)S(1)} collective-permute-done((f32[16,32,4]{2,1,0:T(8,128)S(1)}, f32[16,32,4]{2,1,0:T(8,128)S(1)}, u32[]{:S(2)}, u32[]{:S(2)}) %collective-permute-start.8) | collective-permute-done | bytes 8224 | tf_op jit(solution)/shard_map/ppermute | solution.py:23
  98.1 2.2 %pad_subtract_fusion.29 = (f32[16,32,136]{2,1,0:T(8,128)}, f32[16,32,136]{2,1,0:T(8,128)S(1)}, f32[16,32,136]{2,1,0:T(8,128)}, f32[16,32,136]{2,1,0:T(8,128)}, f32[16,32,136]{2,1,0:T(8,128)}) fusion(f32[16,32,136]{2,1,0:T(8,128)S(1)} %get-tuple-element.18, f32[16,31,136]{2,1,0:T(8,128)S(1)} %get-tuple-element.118, ...), kind=kLoop, calls=%fused_computation.84 | loop fusion | flops 1323008 | bytes 5305344 | tf_op jit(solution)/shard_map/sub | solution.py:72
  102.6 2.2 %collective-permute-start.10 = (f32[4,32,128]{2,1,0:T(8,128)S(1)}, f32[4,32,128]{2,1,0:T(8,128)S(1)}, u32[]{:S(2)}, u32[]{:S(2)}) collective-permute-start(f32[4,32,128]{2,1,0:T(8,128)S(1)} %get-tuple-element.114), channel_id=1, source_target_pairs={{0,4},{4,8},{8,12},{12,16},{16,20},{20,24},{24,28},{1,5},{5,9},{9,... | collective-permute-start | bytes 196616 | tf_op jit(solution)/shard_map/ppermute | solution.py:23
  105.2 3.9 %collective-permute-done.10 = f32[4,32,128]{2,1,0:T(8,128)S(1)} collective-permute-done((f32[4,32,128]{2,1,0:T(8,128)S(1)}, f32[4,32,128]{2,1,0:T(8,128)S(1)}, u32[]{:S(2)}, u32[]{:S(2)}) %collective-permute-start.10) | collective-permute-done | bytes 65568 | tf_op jit(solution)/shard_map/ppermute | solution.py:23
  109.2 2.4 %collective-permute-start.13 = (f32[16,32,4]{2,1,0:T(8,128)S(1)}, f32[16,32,4]{2,1,0:T(8,128)S(1)}, u32[]{:S(2)}, u32[]{:S(2)}) collective-permute-start(f32[16,32,4]{2,1,0:T(8,128)S(1)} %get-tuple-element.176), channel_id=1, source_target_pairs={{1,0},{2,1},{3,2},{5,4},{6,5},{7,6},{9,8},{10,9},{11,10},{13,12},{... | collective-permute-start | bytes 24584 | tf_op jit(solution)/shard_map/ppermute | solution.py:24
  115.6 4.3 %collective-permute-done.12 = f32[16,32,4]{2,1,0:T(8,128)S(1)} collective-permute-done((f32[16,32,4]{2,1,0:T(8,128)S(1)}, f32[16,32,4]{2,1,0:T(8,128)S(1)}, u32[]{:S(2)}, u32[]{:S(2)}) %collective-permute-start.12) | collective-permute-done | bytes 8224 | tf_op jit(solution)/shard_map/ppermute | solution.py:23
  126.5 2.6 %pad_subtract_fusion.21 = (f32[16,32,136]{2,1,0:T(8,128)}, f32[16,32,136]{2,1,0:T(8,128)}, f32[16,32,136]{2,1,0:T(8,128)S(1)}, f32[16,32,136]{2,1,0:T(8,128)}, f...) fusion(f32[16,32,136]{2,1,0:T(8,128)S(1)} %get-tuple-element.37, ...), kind=kLoop, calls=%fused_computation.70 | loop fusion | flops 835584 | bytes 6045184 | tf_op jit(solution)/shard_map/sub | solution.py:72
  129.1 2.4 %fusion.15 = f32[1,8,32,128]{3,2,1,0:T(8,128)S(1)} fusion(f32[16,32,135]{2,1,0:T(8,128)S(1)} %slice.1002, f32[16,32,136]{2,1,0:T(8,128)S(1)} %get-tuple-element.67, f32[16,32,135]{2,1,0:T(8,128)S(1)} %slice.998, f32[16,32,136]{2,1,0:T(8,128)S(1)} %get-tuple-element.65, f32[16,32,136]{2,1,0:T(8,128)} %get-tuple-element.63, f32[16,32,135]{2,1,0:T(8,128)S(1)} %slice.994, ...), kind=kLoop, calls=%fused_computation.111 | loop fusion | flops 884736 | bytes 4687872 | tf_op jit(solution)/shard_map/stack | solution.py:147
  131.5 2.4 %fusion.29 = f32[1,8,32,128]{3,2,1,0:T(8,128)S(1)} fusion(f32[16,31,136]{2,1,0:T(8,128)S(1)} %slice.976, f32[16,32,136]{2,1,0:T(8,128)S(1)} %get-tuple-element.66, f32[16,32,136]{2,1,0:T(8,128)} %get-tuple-element.93, f32[16,31,136]{2,1,0:T(8,128)S(1)} %slice.972, f32[16,32,136]{2,1,0:T(8,128)S(1)} %get-tuple-element.64, ...), kind=kLoop, calls=%fused_computation.138 | loop fusion | flops 884736 | bytes 4641280 | tf_op jit(solution)/shard_map/stack | solution.py:147
  133.9 2.4 %fusion.43 = f32[1,8,32,128]{3,2,1,0:T(8,128)S(1)} fusion(f32[15,32,136]{2,1,0:T(8,128)S(1)} %slice.950, f32[16,32,136]{2,1,0:T(8,128)S(1)} %get-tuple-element.68, f32[16,32,136]{2,1,0:T(8,128)} %get-tuple-element.75, f32[15,32,136]{2,1,0:T(8,128)S(1)} %slice.946, f32[16,32,136]{2,1,0:T(8,128)S(1)} %get-tuple-element.69, ...), kind=kLoop, calls=%fused_computation.165 | loop fusion | flops 884736 | bytes 4580352 | tf_op jit(solution)/shard_map/stack | solution.py:147
  137.2 2.6 %fusion.55 = (f32[8,32,128]{2,1,0:T(8,128)}, f32[8,32,128]{2,1,0:T(8,128)}) fusion(f32[16,32,136]{2,1,0:T(8,128)} %get-tuple-element.38, f32[16,32,136]{2,1,0:T(8,128)S(1)} %get-tuple-element.34, f32[16,32,135]{2,1,0:T(8,128)S(1)} %get-tuple-element.97, f32[16,32,136]{2,1,0:T(8,128)} %get-tuple-element.77, f32[16,32,136]{2,1,0:T(8,128)} %get-tuple-element.91, ...), kind=kLoop, calls=%fused_computation.190 | loop fusion | flops 491520 | bytes 2406400 | tf_op jit(solution)/shard_map/mul | solution.py:140
  (155 shorter events, 61.8 us)
Async XLA Ops:
  0.6 13.1 %copy-start.5 = (f32[8,32,128]{2,1,0:T(8,128)S(1)}, f32[8,32,128]{2,1,0:T(8,128)}, u32[]{:S(2)}) copy-start(f32[8,32,128]{2,1,0:T(8,128)} %param.4) | copy-start | bytes 393220
  1.6 7.4 %collective-permute-start.14 = (f32[4,32,128]{2,1,0:T(8,128)S(1)}, f32[4,32,128]{2,1,0:T(8,128)S(1)}, u32[]{:S(2)}, u32[]{:S(2)}) collective-permute-start(f32[4,32,128]{2,1,0:T(8,128)S(1)} %get-tuple-element.188), channel_id=1, source_target_pairs={{0,4},{4,8},{8,12},{12,16},{16,20},{20,24},{24,28},{1,5},{5,9},{9,... | collective-permute-start | bytes 196616 | tf_op jit(solution)/shard_map/ppermute | solution.py:23
  3.5 6.4 %collective-permute-start.15 = (f32[4,32,128]{2,1,0:T(8,128)S(1)}, f32[4,32,128]{2,1,0:T(8,128)S(1)}, u32[]{:S(2)}, u32[]{:S(2)}) collective-permute-start(f32[4,32,128]{2,1,0:T(8,128)S(1)} %get-tuple-element.187), channel_id=1, source_target_pairs={{4,0},{8,4},{12,8},{16,12},{20,16},{24,20},{28,24},{5,1},{9,5},{13... | collective-permute-start | bytes 196616 | tf_op jit(solution)/shard_map/ppermute | solution.py:24
  10.1 10.0 %collective-permute-start.17 = (f32[16,32,4]{2,1,0:T(8,128)S(1)}, f32[16,32,4]{2,1,0:T(8,128)S(1)}, u32[]{:S(2)}, u32[]{:S(2)}) collective-permute-start(f32[16,32,4]{2,1,0:T(8,128)S(1)} %get-tuple-element.184), channel_id=1, source_target_pairs={{1,0},{2,1},{3,2},{5,4},{6,5},{7,6},{9,8},{10,9},{11,10},{13,12},{... | collective-permute-start | bytes 24584 | tf_op jit(solution)/shard_map/ppermute | solution.py:24
  12.4 10.6 %collective-permute-start.16 = (f32[16,32,4]{2,1,0:T(8,128)S(1)}, f32[16,32,4]{2,1,0:T(8,128)S(1)}, u32[]{:S(2)}, u32[]{:S(2)}) collective-permute-start(f32[16,32,4]{2,1,0:T(8,128)S(1)} %get-tuple-element.183), channel_id=1, source_target_pairs={{0,1},{1,2},{2,3},{4,5},{5,6},{6,7},{8,9},{9,10},{10,11},{12,13},{... | collective-permute-start | bytes 24584 | tf_op jit(solution)/shard_map/ppermute | solution.py:23
  13.8 11.5 %collective-permute-start.1 = (f32[2,5,32,128]{3,2,1,0:T(8,128)S(1)}, f32[2,5,32,128]{3,2,1,0:T(8,128)S(1)}, u32[]{:S(2)}, u32[]{:S(2)}) collective-permute-start(f32[2,5,32,128]{3,2,1,0:T(8,128)S(1)} %get-tuple-element.182), channel_id=1, source_target_pairs={{4,0},{8,4},{12,8},{16,12},{20,16},{24,20},{28,24},{5,1},{9,5},{13... | collective-permute-start | bytes 491528 | tf_op jit(solution)/shard_map/ppermute | solution.py:24
  18.1 7.5 %collective-permute-start = (f32[2,5,32,128]{3,2,1,0:T(8,128)S(1)}, f32[2,5,32,128]{3,2,1,0:T(8,128)S(1)}, u32[]{:S(2)}, u32[]{:S(2)}) collective-permute-start(f32[2,5,32,128]{3,2,1,0:T(8,128)S(1)} %get-tuple-element.181), channel_id=1, source_target_pairs={{0,4},{4,8},{8,12},{12,16},{16,20},{20,24},{24,28},{1,5},{5,9},{9,... | collective-permute-start | bytes 491528 | tf_op jit(solution)/shard_map/ppermute | solution.py:23
  27.8 6.7 %collective-permute-start.3 = (f32[2,18,32,5]{2,0,3,1:T(2,128)}, f32[2,18,32,5]{2,0,3,1:T(2,128)S(1)}, u32[]{:S(2)}, u32[]{:S(2)}) collective-permute-start(f32[2,18,32,5]{2,0,3,1:T(2,128)} %copy.22), channel_id=1, source_target_pairs={{1,0},{2,1},{3,2},{5,4},{6,5},{7,6},{9,8},{10,9},{11,10},{13,12},{... | collective-permute-start | bytes 69128 | tf_op jit(solution)/shard_map/ppermute | solution.py:24
  32.1 6.6 %collective-permute-start.2 = (f32[2,18,32,5]{2,0,3,1:T(2,128)S(1)}, f32[2,18,32,5]{2,0,3,1:T(2,128)}, u32[]{:S(2)}, u32[]{:S(2)}) collective-permute-start(f32[2,18,32,5]{2,0,3,1:T(2,128)S(1)} %copy.21), channel_id=1, source_target_pairs={{0,1},{1,2},{2,3},{4,5},{5,6},{6,7},{8,9},{9,10},{10,11},{12,13},{... | collective-permute-start | bytes 69128 | tf_op jit(solution)/shard_map/ppermute | solution.py:23
  42.0 1.5 %copy-start.7 = (f32[16,32,4]{2,1,0:T(8,128)S(1)}, f32[16,32,4]{2,1,0:T(8,128)}, u32[]{:S(2)}) copy-start(f32[16,32,4]{2,1,0:T(8,128)} %copy-done.6) | copy-start | bytes 24580
  48.2 11.1 %collective-permute-start.4 = (f32[1,32,128]{2,1,0:T(8,128)S(1)}, f32[1,32,128]{2,1,0:T(8,128)S(1)}, u32[]{:S(2)}, u32[]{:S(2)}) collective-permute-start(f32[1,32,128]{2,1,0:T(8,128)S(1)} %slice.804), channel_id=1, source_target_pairs={{0,4},{4,8},{8,12},{12,16},{16,20},{20,24},{24,28},{1,5},{5,9},{9,... | collective-permute-start | bytes 49160 | tf_op jit(solution)/shard_map/ppermute | solution.py:32
  50.2 9.1 %collective-permute-start.5 = (f32[8,32,1]{2,1,0:T(8,128)S(1)}, f32[8,32,1]{2,1,0:T(8,128)S(1)}, u32[]{:S(2)}, u32[]{:S(2)}) collective-permute-start(f32[8,32,1]{2,1,0:T(8,128)S(1)} %slice.811), channel_id=1, source_target_pairs={{0,1},{1,2},{2,3},{4,5},{5,6},{6,7},{8,9},{9,10},{10,11},{12,13},{... | collective-permute-start | bytes 3080 | tf_op jit(solution)/shard_map/ppermute | solution.py:32
  52.8 7.0 %collective-permute-start.19 = (f32[4,32,128]{2,1,0:T(8,128)S(1)}, f32[4,32,128]{2,1,0:T(8,128)S(1)}, u32[]{:S(2)}, u32[]{:S(2)}) collective-permute-start(f32[4,32,128]{2,1,0:T(8,128)S(1)} %get-tuple-element.153), channel_id=1, source_target_pairs={{4,0},{8,4},{12,8},{16,12},{20,16},{24,20},{28,24},{5,1},{9,5},{13... | collective-permute-start | bytes 196616 | tf_op jit(solution)/shard_map/ppermute | solution.py:24
  57.4 6.5 %collective-permute-start.18 = (f32[4,32,128]{2,1,0:T(8,128)S(1)}, f32[4,32,128]{2,1,0:T(8,128)S(1)}, u32[]{:S(2)}, u32[]{:S(2)}) collective-permute-start(f32[4,32,128]{2,1,0:T(8,128)S(1)} %get-tuple-element.152), channel_id=1, source_target_pairs={{0,4},{4,8},{8,12},{12,16},{16,20},{20,24},{24,28},{1,5},{5,9},{9,... | collective-permute-start | bytes 196616 | tf_op jit(solution)/shard_map/ppermute | solution.py:23
  64.0 10.1 %collective-permute-start.21 = (f32[16,32,4]{2,1,0:T(8,128)S(1)}, f32[16,32,4]{2,1,0:T(8,128)S(1)}, u32[]{:S(2)}, u32[]{:S(2)}) collective-permute-start(f32[16,32,4]{2,1,0:T(8,128)S(1)} %get-tuple-element.180), channel_id=1, source_target_pairs={{1,0},{2,1},{3,2},{5,4},{6,5},{7,6},{9,8},{10,9},{11,10},{13,12},{... | collective-permute-start | bytes 24584 | tf_op jit(solution)/shard_map/ppermute | solution.py:24
  68.3 8.3 %collective-permute-start.20 = (f32[16,32,4]{2,1,0:T(8,128)S(1)}, f32[16,32,4]{2,1,0:T(8,128)S(1)}, u32[]{:S(2)}, u32[]{:S(2)}) collective-permute-start(f32[16,32,4]{2,1,0:T(8,128)S(1)} %get-tuple-element.179), channel_id=1, source_target_pairs={{0,1},{1,2},{2,3},{4,5},{5,6},{6,7},{8,9},{9,10},{10,11},{12,13},{... | collective-permute-start | bytes 24584 | tf_op jit(solution)/shard_map/ppermute | solution.py:23
  69.6 11.6 %collective-permute-start.7 = (f32[4,32,128]{2,1,0:T(8,128)S(1)}, f32[4,32,128]{2,1,0:T(8,128)S(1)}, u32[]{:S(2)}, u32[]{:S(2)}) collective-permute-start(f32[4,32,128]{2,1,0:T(8,128)S(1)} %get-tuple-element.186), channel_id=1, source_target_pairs={{4,0},{8,4},{12,8},{16,12},{20,16},{24,20},{28,24},{5,1},{9,5},{13... | collective-permute-start | bytes 196616 | tf_op jit(solution)/shard_map/ppermute | solution.py:24
  71.5 9.7 %collective-permute-start.6 = (f32[4,32,128]{2,1,0:T(8,128)S(1)}, f32[4,32,128]{2,1,0:T(8,128)S(1)}, u32[]{:S(2)}, u32[]{:S(2)}) collective-permute-start(f32[4,32,128]{2,1,0:T(8,128)S(1)} %get-tuple-element.185), channel_id=1, source_target_pairs={{0,4},{4,8},{8,12},{12,16},{16,20},{20,24},{24,28},{1,5},{5,9},{9,... | collective-permute-start | bytes 196616 | tf_op jit(solution)/shard_map/ppermute | solution.py:23
  81.4 7.9 %collective-permute-start.9 = (f32[16,32,4]{2,1,0:T(8,128)S(1)}, f32[16,32,4]{2,1,0:T(8,128)S(1)}, u32[]{:S(2)}, u32[]{:S(2)}) collective-permute-start(f32[16,32,4]{2,1,0:T(8,128)S(1)} %get-tuple-element.178), channel_id=1, source_target_pairs={{1,0},{2,1},{3,2},{5,4},{6,5},{7,6},{9,8},{10,9},{11,10},{13,12},{... | collective-permute-start | bytes 24584 | tf_op jit(solution)/shard_map/ppermute | solution.py:24
  83.8 9.7 %collective-permute-start.8 = (f32[16,32,4]{2,1,0:T(8,128)S(1)}, f32[16,32,4]{2,1,0:T(8,128)S(1)}, u32[]{:S(2)}, u32[]{:S(2)}) collective-permute-start(f32[16,32,4]{2,1,0:T(8,128)S(1)} %get-tuple-element.177), channel_id=1, source_target_pairs={{0,1},{1,2},{2,3},{4,5},{5,6},{6,7},{8,9},{9,10},{10,11},{12,13},{... | collective-permute-start | bytes 24584 | tf_op jit(solution)/shard_map/ppermute | solution.py:23
  100.4 4.8 %collective-permute-start.11 = (f32[4,32,128]{2,1,0:T(8,128)S(1)}, f32[4,32,128]{2,1,0:T(8,128)S(1)}, u32[]{:S(2)}, u32[]{:S(2)}) collective-permute-start(f32[4,32,128]{2,1,0:T(8,128)S(1)} %get-tuple-element.115), channel_id=1, source_target_pairs={{4,0},{8,4},{12,8},{16,12},{20,16},{24,20},{28,24},{5,1},{9,5},{13... | collective-permute-start | bytes 196616 | tf_op jit(solution)/shard_map/ppermute | solution.py:24
  102.6 6.5 %collective-permute-start.10 = (f32[4,32,128]{2,1,0:T(8,128)S(1)}, f32[4,32,128]{2,1,0:T(8,128)S(1)}, u32[]{:S(2)}, u32[]{:S(2)}) collective-permute-start(f32[4,32,128]{2,1,0:T(8,128)S(1)} %get-tuple-element.114), channel_id=1, source_target_pairs={{0,4},{4,8},{8,12},{12,16},{16,20},{20,24},{24,28},{1,5},{5,9},{9,... | collective-permute-start | bytes 196616 | tf_op jit(solution)/shard_map/ppermute | solution.py:23
  109.2 6.4 %collective-permute-start.13 = (f32[16,32,4]{2,1,0:T(8,128)S(1)}, f32[16,32,4]{2,1,0:T(8,128)S(1)}, u32[]{:S(2)}, u32[]{:S(2)}) collective-permute-start(f32[16,32,4]{2,1,0:T(8,128)S(1)} %get-tuple-element.176), channel_id=1, source_target_pairs={{1,0},{2,1},{3,2},{5,4},{6,5},{7,6},{9,8},{10,9},{11,10},{13,12},{... | collective-permute-start | bytes 24584 | tf_op jit(solution)/shard_map/ppermute | solution.py:24
  111.6 8.3 %collective-permute-start.12 = (f32[16,32,4]{2,1,0:T(8,128)S(1)}, f32[16,32,4]{2,1,0:T(8,128)S(1)}, u32[]{:S(2)}, u32[]{:S(2)}) collective-permute-start(f32[16,32,4]{2,1,0:T(8,128)S(1)} %get-tuple-element.175), channel_id=1, source_target_pairs={{0,1},{1,2},{2,3},{4,5},{5,6},{6,7},{8,9},{9,10},{10,11},{12,13},{... | collective-permute-start | bytes 24584 | tf_op jit(solution)/shard_map/ppermute | solution.py:23
  (8 other events, 8.1 us)
where the time goes:
time: 141 us; the launch traced here: 140 us
  starting transfers between devices  53.2 us (38%)
  other arithmetic  37.4 us (27%)
  waiting for transfers between devices  28.9 us (20%)
  local copies, waits for them, and re-layouts  18.6 us (13%)
  between operations  1.57 us (1%)
    ppermute x10, starting transfers between devices, extended_2(): after = lax.ppermute(initial, axis, down)  32.8 us
    ppermute x10, waiting for transfers between devices, extended_2(): before = lax.ppermute(last, axis, up)  26 us
    ppermute x10, starting transfers between devices, extended_2(): before = lax.ppermute(last, axis, up)  17.2 us
    slice x57, local copies, waits for them, and re-layouts, shift_up(): lax.slice_in_dim(array, 1, length, axis=axis_dim)  8.69 us
    add x6, other arithmetic, forward_sweep(): field + inside * (weight * (source - apply_operator(field, upper, lower))...  8.6 us
    another operation x4, other arithmetic, per_device(): return (grad_source, adjoint_int, jnp.stack(grad_faces))  8.03 us
    sub x4, other arithmetic, apply_operator(): applied = applied + upper[axis_dim] * (field - shift_up(field, axis_dim))  7.23 us
    div x6, other arithmetic, per_device(): ratio = scaled * residual_ext / diag_safe  7.09 us
  transfers between devices with their start and end apart: 22, of which 10 were waited for; matrix products, arithmetic and copies ran while one was open for 11% of the time, Pallas kernels for 0%

commit v1 on v0

v1 whole, which is shorter than its diff:
```python
import math

import jax
import jax.numpy as jnp
from jax import lax
from jax.experimental import pallas as pl
from jax.experimental.pallas import tpu as pltpu
from jax.sharding import PartitionSpec as P

SWEEPS = 6

gas_density = 0.25
lower_bound = 0.25
upper_bound = 2.0

FACE = (1.0, 2.0 / (1.0 + gas_density), 1.0 / gas_density)


def chebyshev_weights(count):
    center = 0.5 * (upper_bound + lower_bound)
    radius = 0.5 * (upper_bound - lower_bound)
    roots = [
        center + radius * math.cos(math.pi * (2 * number + 1) / (2 * count))
        for number in range(count)
    ]
    order = []
    for number in range(count // 2):
        order.append(number)
        order.append(count - 1 - number)
    return [1.0 / roots[position] for position in order]


def face(pair):
    return jnp.where(pair < 0.5, FACE[0], jnp.where(pair < 1.5, FACE[1], FACE[2]))


def iota(dim):
    return lax.broadcasted_iota(jnp.int32, (32, 128), dim)


def y_up(v):
    return pltpu.roll(v, v.shape[0] - 1, 0)


def y_down(v):
    return pltpu.roll(v, 1, 0)


def z_up(v):
    return pltpu.roll(v, v.shape[1] - 1, 1)


def z_down(v):
    return pltpu.roll(v, 1, 1)


HALO = SWEEPS + 1
PLANES = 2 * HALO + 2 * SWEEPS
ROWS = 32
CORNER = 2 * ROWS + 8


def pack_kernel(where_ref, ph_ref, dv_ref, p_ref, vc_ref, xa_ref, xb_ref, za_ref, zb_ref, row_ref, adj_ref, up_ref, down_ref):
    cells_x = ph_ref.shape[0]
    x_even = where_ref[0] % 2 == 0
    z_even = where_ref[2] % 2 == 0
    lane = iota(1)
    row = iota(0)
    before = None
    for i in range(cells_x):
        ph = ph_ref[i].astype(jnp.float32)
        adj = jnp.zeros_like(ph)
        if before is not None:
            adj = adj - before
        if i + 1 < cells_x:
            before = face(ph + ph_ref[i + 1].astype(jnp.float32)) * vc_ref[0, i]
            adj = adj + before
        flux = face(ph + jnp.where(row == ph.shape[0] - 1, ph, y_up(ph))) * vc_ref[1, i]
        adj = adj + flux - jnp.where(row == 0, 0.0, y_down(flux))
        flux = jnp.where(lane == ph.shape[1] - 1, 0.0, face(ph + z_up(ph)) * vc_ref[2, i])
        adj = adj + flux - z_down(flux)
        adj_ref[i] = adj

    first = cells_x - HALO
    n = SWEEPS

    def upward(out):
        out[0:HALO] = ph_ref[first:].astype(jnp.float32)
        out[HALO : HALO + n] = dv_ref[first + 1 :]
        out[HALO + n : HALO + 2 * n] = adj_ref[first + 1 :]
        out[HALO + 2 * n : HALO + 3 * n] = p_ref[first + 1 :]
        out[HALO + 3 * n] = vc_ref[0, cells_x - 1]

    def downward(out):
        out[0:HALO] = ph_ref[0:HALO].astype(jnp.float32)
        out[HALO : HALO + n] = dv_ref[0:n]
        out[HALO + n : HALO + 2 * n] = adj_ref[0:n]
        out[HALO + 2 * n : 2 * HALO + 2 * n] = p_ref[0:HALO]

    @pl.when(x_even)
    def _():
        upward(xa_ref)
        downward(xb_ref)

    @pl.when(jnp.logical_not(x_even))
    def _():
        upward(xb_ref)
        downward(xa_ref)

    cells = cells_x * ph_ref.shape[1]
    width = ph_ref.shape[2]

    def turned(v):
        return v.reshape(cells, width).T

    t = turned(ph_ref[...].astype(jnp.float32))
    up_ref[0:HALO] = t[width - HALO :]
    down_ref[0:HALO] = t[0:HALO]
    t = turned(dv_ref[...])
    up_ref[HALO : HALO + n] = t[width - n :]
    down_ref[HALO : HALO + n] = t[0:n]
    t = turned(adj_ref[...])
    up_ref[HALO + n : HALO + 2 * n] = t[width - n :]
    down_ref[HALO + n : HALO + 2 * n] = t[0:n]
    t = turned(p_ref[...])
    up_ref[HALO + 2 * n : HALO + 3 * n] = t[width - n :]
    down_ref[HALO + 2 * n : 2 * HALO + 2 * n] = t[0:HALO]
    t = turned(vc_ref[2])
    up_ref[HALO + 3 * n : HALO + 3 * n + 1] = t[width - 1 :]
    row_ref[...] = t[width - 8 :]
    t = turned(vc_ref[0])
    up_ref[2 * HALO + 2 * n + 0 : 2 * HALO + 3 * n] = t[width - n :]
    down_ref[2 * HALO + 2 * n : 2 * HALO + 3 * n] = t[0:n]

    @pl.when(z_even)
    def _():
        za_ref[...] = up_ref[...]
        zb_ref[...] = down_ref[...]

    @pl.when(jnp.logical_not(z_even))
    def _():
        zb_ref[...] = up_ref[...]
        za_ref[...] = down_ref[...]


def unpack_kernel(where_ref, own_ref, ca_ref, cb_ref, h_ref, v_ref, e_ref, t_ref):
    x_even = where_ref[0] % 2 == 0
    z_even = where_ref[2] % 2 == 0
    n = SWEEPS
    width = t_ref.shape[1]
    cells = own_ref.shape[1]
    t_ref[...] = jnp.zeros_like(t_ref)
    for block in range(3):
        if block == 1:
            part = own_ref[...]
        else:
            low_is_a = jnp.logical_not(x_even) if block == 0 else x_even
            part = jnp.where(low_is_a, ca_ref[...], cb_ref[...])
        zl = jnp.where(z_even, part[ROWS : 2 * ROWS], part[0:ROWS])
        zh = jnp.where(z_even, part[0:ROWS], part[ROWS : 2 * ROWS])
        at = slice(block * cells, (block + 1) * cells)
        t_ref[0, 0:HALO, at] = zh[0:HALO]
        t_ref[0, width - HALO :, at] = zl[0:HALO]
        for field in (1, 2):
            first = HALO + (field - 1) * n
            t_ref[field, 0:n, at] = zh[first : first + n]
            t_ref[field, width - n :, at] = zl[first : first + n]
        first = HALO + 2 * n
        t_ref[3, 0:HALO, at] = zh[first : first + HALO]
        t_ref[3, width - n :, at] = zl[first : first + n]
        t_ref[4, width - 1 :, at] = zl[first + n : first + n + 1]
        t_ref[4, width // 2 - 1 : width // 2, at] = part[2 * ROWS + 7 : 2 * ROWS + 8]
        t_ref[5, 0:n, at] = zh[2 * HALO + 2 * n :]
        t_ref[5, width - n :, at] = zl[2 * HALO + 2 * n :]
    planes = h_ref.shape[1]
    for field in range(4):
        h_ref[field] = t_ref[field].T.reshape(planes, cells * 3 // planes, width)
    v_ref[...] = t_ref[4].T.reshape(planes, cells * 3 // planes, width)
    third = planes // 3
    own = t_ref[5].T.reshape(planes, cells * 3 // planes, width)
    e_ref[0] = own[third - 1]
    e_ref[1] = own[2 * third - 1]


def main_kernel(
    where_ref, ph_ref, dv_ref, p_ref, vc_ref, adj_ref, xa_ref, xb_ref, h_ref, v_ref, e_ref,
    gd_ref, gp_ref, gf_ref,
    e1, e2, f0_ref, c_ref, s_ref, ps, us, diag_ref, r_ref,
):
    cells_x, ny, width = ph_ref.shape
    n = SWEEPS
    off = cells_x
    wi = where_ref[0]
    x_first = wi == 0
    x_last = wi == where_ref[1] - 1
    z_first = where_ref[2] == 0
    z_last = where_ref[2] == where_ref[3] - 1
    x_even = wi % 2 == 0
    lane = iota(1)
    row = iota(0)
    lane0 = lane == 0
    lane_end = lane == width - 1
    weights = chebyshev_weights(SWEEPS)

    def low(k):
        return jnp.where(x_even, xb_ref[k], xa_ref[k])

    def high(k):
        return jnp.where(x_even, xa_ref[k], xb_ref[k])

    for i in range(cells_x):
        e1[i + off] = ph_ref[i].astype(jnp.float32)
    for k in range(HALO):
        e1[off - HALO + k] = low(k)
        e1[off + cells_x + k] = high(k)
    e1[off - 1] = jnp.where(x_first, e1[off], e1[off - 1])
    e1[off + cells_x] = jnp.where(x_last, e1[off + cells_x - 1], e1[off + cells_x])
    for i in range(-HALO, cells_x + HALO):
        e2[i + off] = h_ref[0, i + off]
    e2[off - 1] = jnp.where(x_first, e2[off], e2[off - 1])
    e2[off + cells_x] = jnp.where(x_last, e2[off + cells_x - 1], e2[off + cells_x])
    at_low = jnp.logical_and(lane_end, z_first)
    at_high = jnp.logical_and(lane0, z_last)
    for i in range(-HALO, cells_x + HALO):
        ph1 = e1[i + off]
        e2[i + off] = jnp.where(at_high, z_down(ph1), jnp.where(at_low, z_up(ph1), e2[i + off]))

    in_low = jnp.logical_not(x_first)
    in_high = jnp.logical_not(x_last)
    side_high = jnp.logical_and(lane <= HALO - 1, jnp.logical_not(z_last))
    side_low = jnp.logical_and(lane >= width - HALO, jnp.logical_not(z_first))
    side = jnp.logical_or(side_low, side_high)
    core = jnp.logical_and(
        side, jnp.logical_or(lane < HALO - 1, lane > width - HALO)
    )

    def within(i):
        return in_low if i < 0 else (in_high if i >= cells_x else None)

    def masked(i, col, value, cover):
        flag = within(i)
        if col == 0:
            return value if flag is None else jnp.where(flag, value, 0.0)
        return jnp.where(cover if flag is None else jnp.logical_and(cover, flag), value, 0.0)

    for i in range(-n, cells_x + HALO):
        if i < 0:
            value = low(HALO + 2 * n + n + i)
        elif i >= cells_x:
            value = high(HALO + 2 * n + i - cells_x)
        else:
            value = p_ref[i]
        ps[0, 0, i + off] = masked(i, 0, value, None)
        ps[0, 1, i + off] = masked(i, 1, h_ref[3, i + off], side)

    for i in range(-HALO, cells_x + n):
        f0_ref[0, i + off] = face(e1[i + off] + e1[i + 1 + off])
        f0_ref[1, i + off] = face(e2[i + off] + e2[i + 1 + off])

    cross = {}
    for number, i in enumerate((-1, cells_x - 1)):
        value = low(HALO + 3 * n) if i < 0 else vc_ref[0, i]
        flux = (f0_ref[0, i + off] * value, f0_ref[1, i + off] * e_ref[number])
        cross[i] = tuple(jnp.where(in_low, v, 0.0) for v in flux) if i < 0 else flux

    for i in range(-n, cells_x + n):
        j = i + off
        ph = (e1[j], e2[j])
        up_z = [z_up(v) for v in ph]
        f2 = [
            face(ph[0] + jnp.where(lane_end, up_z[1], up_z[0])),
            face(ph[1] + jnp.where(lane_end, up_z[0], up_z[1])),
        ]
        down_z = [z_down(v) for v in f2]
        l2 = [jnp.where(lane0, down_z[1], down_z[0]), jnp.where(lane0, down_z[0], down_z[1])]
        if 0 <= i < cells_x:
            last = vc_ref[2, i]
        else:
            last = pltpu.roll(v_ref[j], width // 2, 1)
        g = [
            jnp.where(lane_end, f2[0] * last, 0.0),
            jnp.where(jnp.logical_and(lane_end, jnp.logical_not(z_first)), f2[1] * v_ref[j], 0.0),
        ]
        down_g = [z_down(v) for v in g]
        for col in range(2):
            f1 = face(ph[col] + jnp.where(row == ny - 1, ph[col], y_up(ph[col])))
            l1 = face(ph[col] + jnp.where(row == 0, ph[col], y_down(ph[col])))
            f0 = f0_ref[col, j]
            l0 = f0_ref[col, j - 1]
            diag = f0 + l0 + f1 + l1 + f2[col] + l2[col]
            inv = masked(i, col, 1.0 / diag, core)
            if col == 0 and 0 <= i < cells_x:
                diag_ref[i] = diag
            c_ref[0, col, j] = f0 * inv
            c_ref[1, col, j] = l0 * inv
            c_ref[2, col, j] = jnp.where(row == ny - 1, 0.0, f1 * inv)
            c_ref[3, col, j] = jnp.where(row == 0, 0.0, l1 * inv)
            c_ref[4, col, j] = f2[col] * inv
            c_ref[5, col, j] = l2[col] * inv
            if col == 1:
                source = h_ref[1, j]
                adj = h_ref[2, j]
            elif i < 0:
                source = low(HALO + n + i)
                adj = low(HALO + n + n + i)
            elif i >= cells_x:
                source = high(HALO + i - cells_x)
                adj = high(HALO + n + i - cells_x)
            else:
                source = dv_ref[i]
                adj = adj_ref[i]
            if i in cross:
                adj = adj + cross[i][col]
            if i - 1 in cross:
                adj = adj - cross[i - 1][col]
            adj = adj + g[col] - down_g[1 - col]
            keep = masked(i, col, jnp.ones_like(inv), core) > 0.5
            s_ref[col, j] = jnp.where(keep, source, 0.0) * inv
            us[0, col, j] = jnp.where(keep, adj, 0.0) * inv

    def spread(state, k, col, j):
        v = (state[k, 0, j], state[k, 1, j])
        up = jnp.where(lane_end, z_up(v[1 - col]), z_up(v[col]))
        down = jnp.where(lane0, z_down(v[1 - col]), z_down(v[col]))
        total = c_ref[0, col, j] * state[k, col, j + 1] + c_ref[1, col, j] * state[k, col, j - 1]
        total = total + c_ref[2, col, j] * y_up(v[col]) + c_ref[3, col, j] * y_down(v[col])
        return total + c_ref[4, col, j] * up + c_ref[5, col, j] * down

    us[0, 0, off + cells_x + n] = jnp.zeros((ny, width), jnp.float32)
    us[0, 1, off + cells_x + n] = jnp.zeros((ny, width), jnp.float32)
    us[0, 0, off - n - 1] = jnp.zeros((ny, width), jnp.float32)
    us[0, 1, off - n - 1] = jnp.zeros((ny, width), jnp.float32)
    for k in range(n):
        w = weights[k]
        wu = weights[n - 1 - k]
        for i in range(-(n - 1) + k, cells_x + n - k):
            j = i + off
            for col in range(2):
                p = ps[k, col, j]
                ps[k + 1, col, j] = (1.0 - w) * p + w * (s_ref[col, j] + spread(ps, k, col, j))
                if i < cells_x + n - 1 - k:
                    u = us[k, col, j]
                    us[k + 1, col, j] = (1.0 - wu) * u + wu * spread(us, k, col, j)

    for i in range(cells_x + 1):
        j = i + off
        for col in range(2):
            total = jnp.zeros((ny, width), jnp.float32)
            for k in range(n):
                total = total + us[n - 1 - k, col, j] * (ps[k + 1, col, j] - ps[k, col, j])
            r_ref[col, j] = total
    for i in range(cells_x):
        j = i + off
        gp_ref[i] = us[n, 0, j] * diag_ref[i]
        gd = jnp.zeros((ny, width), jnp.float32)
        terms = [jnp.zeros((ny, width), jnp.float32) for _ in range(3)]

        def rises(v, x_next, v2):
            z_next = jnp.where(lane_end, z_up(v2), z_up(v))
            y_next = jnp.where(row == ny - 1, 0.0, y_up(v))
            return x_next - v, y_next - v, z_next - v

        for k in range(n):
            u = us[n - 1 - k, 0, j]
            gd = gd + weights[k] * u
            p = ps[k, 0, j]
            rise_u = rises(u, us[n - 1 - k, 0, j + 1], us[n - 1 - k, 1, j])
            rise_p = rises(p, ps[k, 0, j + 1], ps[k, 1, j])
            for a in range(3):
                terms[a] = terms[a] + weights[k] * (rise_u[a] * rise_p[a])
        gd_ref[i] = gd
        p = ps[n, 0, j]
        rise = rises(p, ps[n, 0, j + 1], ps[n, 1, j])
        r = r_ref[0, j]
        y_next = jnp.where(row == ny - 1, 0.0, y_up(r))
        z_next = jnp.where(lane_end, z_up(r_ref[1, j]), z_up(r))
        nexts = (r_ref[0, j + 1], y_next, z_next)
        for a in range(3):
            gf_ref[a, i] = -vc_ref[a, i] * rise[a] - terms[a] - (r + nexts[a])


def swaps(size, other, odd, spare_first):
    pairs = []
    for i in range(size):
        for k in range(other):
            partner = ((i + 1) ^ 1) - 1 if odd else i ^ 1
            target = (partner, k) if 0 <= partner < size else (i, k ^ 1)
            source = (i, k)
            pairs.append((source, target))
    return pairs


def flat_pairs(pairs, narrow, turned):
    def flat(at):
        return at[1] * narrow + at[0] if turned else at[0] * narrow + at[1]

    return [(flat(source), flat(target)) for source, target in pairs]


def per_device(divergence, pressure_start, phase, velocity_cot):
    cells_x, ny, cells_z = divergence.shape
    wide, narrow = lax.axis_size("wide"), lax.axis_size("narrow")
    axes = ("wide", "narrow")
    x_even = flat_pairs(swaps(wide, narrow, False, True), narrow, False)
    x_odd = flat_pairs(swaps(wide, narrow, True, True), narrow, False)
    z_even = flat_pairs(swaps(narrow, wide, False, True), narrow, True)
    z_odd = flat_pairs(swaps(narrow, wide, True, True), narrow, True)
    at = jnp.stack(
        [lax.axis_index("wide"), jnp.int32(wide), lax.axis_index("narrow"), jnp.int32(narrow)]
    ).astype(jnp.int32)

    f32 = jnp.float32
    smem = pl.BlockSpec(memory_space=pltpu.SMEM)
    vmem = pl.BlockSpec(memory_space=pltpu.VMEM)

    def shape(*dims):
        return jax.ShapeDtypeStruct(dims, f32)

    slots = 2 * HALO + 2 * SWEEPS
    cells = cells_x * ny
    xa, xb, za, zb, edge, adj = pl.pallas_call(
        pack_kernel,
        out_shape=(
            shape(slots, ny, cells_z), shape(slots, ny, cells_z), shape(ROWS, cells), shape(ROWS, cells),
            shape(8, cells), shape(cells_x, ny, cells_z),
        ),
        in_specs=[smem] + [vmem] * 4,
        out_specs=(vmem,) * 6,
        scratch_shapes=[pltpu.VMEM((ROWS, cells), f32)] * 2,
        name="pack",
    )(at, phase, divergence, pressure_start, velocity_cot)

    got_xb = lax.ppermute(xb, axes, x_odd)
    got_xa = lax.ppermute(xa, axes, x_even)
    got_za = lax.ppermute(za, axes, z_even)
    got_zb = lax.ppermute(zb, axes, z_odd)
    corner = jnp.concatenate([got_za, got_zb, edge], axis=0)
    got_cb = lax.ppermute(corner, axes, x_odd)
    got_ca = lax.ppermute(corner, axes, x_even)

    total = 3 * cells_x
    sides, flux_z, flux_x = pl.pallas_call(
        unpack_kernel,
        out_shape=(shape(4, total, ny, cells_z), shape(total, ny, cells_z), shape(2, ny, cells_z)),
        in_specs=[smem] + [vmem] * 3,
        out_specs=(vmem,) * 3,
        scratch_shapes=[pltpu.VMEM((6, cells_z, 3 * cells), f32)],
        name="unpack",
    )(at, corner, got_ca, got_cb)

    block = (total, ny, cells_z)
    return pl.pallas_call(
        main_kernel,
        out_shape=(
            shape(cells_x, ny, cells_z), shape(cells_x, ny, cells_z), shape(3, cells_x, ny, cells_z),
        ),
        in_specs=[smem] + [vmem] * 10,
        out_specs=(vmem,) * 3,
        scratch_shapes=[
            pltpu.VMEM(block, f32),
            pltpu.VMEM(block, f32),
            pltpu.VMEM((2, *block), f32),
            pltpu.VMEM((6, 2, *block), f32),
            pltpu.VMEM((2, *block), f32),
            pltpu.VMEM((SWEEPS + 1, 2, *block), f32),
            pltpu.VMEM((SWEEPS + 1, 2, *block), f32),
            pltpu.VMEM((cells_x, ny, cells_z), f32),
            pltpu.VMEM((2, *block), f32),
        ],
        name="sweeps",
    )(at, phase, divergence, pressure_start, velocity_cot, adj, got_xa, got_xb, sides, flux_z, flux_x)


def solution(mesh):
    in_specs = (
        P("wide", None, "narrow"),
        P("wide", None, "narrow"),
        P("wide", None, "narrow"),
        P(None, "wide", None, "narrow"),
    )
    out_specs = (
        P("wide", None, "narrow"),
        P("wide", None, "narrow"),
        P(None, "wide", None, "narrow"),
    )
    return jax.shard_map(
        per_device, mesh=mesh, in_specs=in_specs, out_specs=out_specs, check_vma=False
    )
```

time: 141 us -> 38.2 us (0.27)
  the two profiles are of different devices: /device:TPU:28 before, /device:TPU:1 now
where the time goes in v1:
time: 38.2 us; the launch traced here: 38 us
  Pallas kernels  17.9 us (47%)
  starting transfers between devices  8.13 us (21%)
  waiting for transfers between devices  7.86 us (21%)
  local copies, waits for them, and re-layouts  2.87 us (8%)
  between operations  0.66 us (2%)
  other arithmetic  0.59 us (2%)
    pallas_call x1, Pallas kernels, per_device(): pl.pallas_call(main_kernel, out_shape=(shape(cells_x, ny, cells_z), shape...  12.4 us
    ppermute x1, waiting for transfers between devices, per_device(): got_cb = lax.ppermute(corner, axes, x_odd)  6.44 us
    pallas_call x1, Pallas kernels, per_device(): pl.pallas_call(unpack_kernel, out_shape=(shape(4, total, ny, cells_z), sh...  2.77 us
    ppermute x1, starting transfers between devices, per_device(): got_ca = lax.ppermute(corner, axes, x_even)  2.71 us
    pallas_call x1, Pallas kernels, per_device(): pl.pallas_call(pack_kernel, out_shape=(shape(slots, ny, cells_z), shape(s...  2.69 us
    unnamed x12, local copies, waits for them, and re-layouts  2.17 us
    ppermute x1, starting transfers between devices, per_device(): got_za = lax.ppermute(za, axes, z_even)  2.11 us
    ppermute x1, waiting for transfers between devices, per_device(): got_zb = lax.ppermute(zb, axes, z_odd)  1.41 us
  transfers between devices with their start and end apart: 6, of which 2 were waited for; matrix products, arithmetic and copies ran while one was open for 2% of the time, Pallas kernels for 7%

profile of v1, /device:TPU:1, one launch (start us, length us, event | category | flops | bytes accessed | tf_op | source)
XLA Modules:
  0.0 38.0 jit_solution(7748057552614077807)
XLA Ops:
  0.6 0.6 %pad_add_fusion.where_ref = s32[4]{0:T(128)} fusion(s32[1]{0:T(128)} %constant.12.clone.1, s32[1]{0:T(128)} %bitcast.1, s32[1]{0:T(128)} %constant.10.clone.1, s32[1]{0:T(128)} %bitcast), kind=kLoop, calls=%fused_computation.3 | loop fusion | flops 12 | bytes 32 | tf_op jit(solution)/shard_map/stack | solution.py:408
  1.2 2.7 %pack.1 = (f32[26,32,128]{2,1,0:T(8,128)}, f32[26,32,128]{2,1,0:T(8,128)}, f32[32,256]{1,0:T(8,128)}, f32[32,256]{1,0:T(8,128)}, f32[8,256]{1,0:T(8,128)}, /*index=5*/f32[8,32,128]{2,1,0:T(8,128)}) custom-call(s32[4]{0:T(128)} %pad_add_fusion.where_ref, s32[8,32,128]{2,1,0:T(8,128)} %ph_ref.3, f32[8,32,128]{2,1,0:T(8,128)} %dv_ref.3, f32[8,32,128]{2,1,0:T(8,128)} %p_ref.3, ...), custom_call_target="tpu_custom_call" | custom-call | tf_op jit(solution)/shard_map/pack/pallas_call | solution.py:421
  3.9 2.1 %collective-permute-start.2 = (f32[32,256]{1,0:T(8,128)}, f32[32,256]{1,0:T(8,128)S(1)}, u32[]{:S(2)}, u32[]{:S(2)}) collective-permute-start(f32[32,256]{1,0:T(8,128)} %get-tuple-element.15), channel_id=1, source_target_pairs={{0,1},{4,5},{8,9},{12,13},{16,17},{20,21},{24,25},{28,29},{1,0},{5... | collective-permute-start | bytes 98312 | tf_op jit(solution)/shard_map/ppermute | solution.py:435
  6.0 0.9 %collective-permute-start = (f32[26,32,128]{2,1,0:T(8,128)}, f32[26,32,128]{2,1,0:T(8,128)S(1)}, u32[]{:S(2)}, u32[]{:S(2)}) collective-permute-start(f32[26,32,128]{2,1,0:T(8,128)} %get-tuple-element.13), channel_id=1, source_target_pairs={{0,4},{1,5},{2,6},{3,7},{4,0},{5,1},{6,2},{7,3},{8,12},{9,13},{10,... | collective-permute-start | bytes 1277960 | tf_op jit(solution)/shard_map/ppermute | solution.py:434
  7.0 1.1 %collective-permute-start.1 = (f32[26,32,128]{2,1,0:T(8,128)}, f32[26,32,128]{2,1,0:T(8,128)S(1)}, u32[]{:S(2)}, u32[]{:S(2)}) collective-permute-start(f32[26,32,128]{2,1,0:T(8,128)} %get-tuple-element.14), channel_id=1, source_target_pairs={{0,1},{1,0},{2,3},{3,2},{4,8},{5,9},{6,10},{7,11},{8,4},{9,5},{10,... | collective-permute-start | bytes 1277960 | tf_op jit(solution)/shard_map/ppermute | solution.py:433
  8.1 0.0 collective-permute-start.3
  8.1 0.0 collective-permute-done.2
  8.1 1.4 %collective-permute-done.3 = f32[32,256]{1,0:T(8,128)S(1)} collective-permute-done((f32[32,256]{1,0:T(8,128)}, f32[32,256]{1,0:T(8,128)S(1)}, u32[]{:S(2)}, u32[]{:S(2)}) %collective-permute-start.3) | collective-permute-done | bytes 32800 | tf_op jit(solution)/shard_map/ppermute | solution.py:436
  9.5 0.7 %constant_dynamic-update-slice_fusion.own_ref = f32[72,256]{1,0:T(8,128)S(1)} fusion(f32[72,256]{1,0:T(8,128)S(1)} %constant_dynamic-update-slice_fusion.1, f32[8,256]{1,0:T(8,128)} %get-tuple-element.17), kind=kLoop, calls=%fused_computation | loop fusion | bytes 16384 | tf_op jit(solution)/shard_map/concatenate | solution.py:437
  10.2 0.0 copy-start.2
  10.2 1.3 %collective-permute-start.5 = (f32[72,256]{1,0:T(8,128)S(1)}, f32[72,256]{1,0:T(8,128)S(1)}, u32[]{:S(2)}, u32[]{:S(2)}) collective-permute-start(f32[72,256]{1,0:T(8,128)S(1)} %constant_dynamic-update-slice_fusion.own_ref), channel_id=1, source_target_pairs={{0,1},{1,0},{2,3},{3,2},{4,8},{5,9},{6,10},{7,11},{8,4},{9,5},{10,... | collective-permute-start | bytes 221192 | tf_op jit(solution)/shard_map/ppermute | solution.py:438
  11.5 2.7 %collective-permute-start.4 = (f32[72,256]{1,0:T(8,128)S(1)}, f32[72,256]{1,0:T(8,128)S(1)}, u32[]{:S(2)}, u32[]{:S(2)}) collective-permute-start(f32[72,256]{1,0:T(8,128)S(1)} %constant_dynamic-update-slice_fusion.own_ref), channel_id=1, source_target_pairs={{0,4},{1,5},{2,6},{3,7},{4,0},{5,1},{6,2},{7,3},{8,12},{9,13},{10,... | collective-permute-start | bytes 221192 | tf_op jit(solution)/shard_map/ppermute | solution.py:439
  14.2 6.4 %collective-permute-done.5.cb_ref = f32[72,256]{1,0:T(8,128)S(1)} collective-permute-done((f32[72,256]{1,0:T(8,128)S(1)}, f32[72,256]{1,0:T(8,128)S(1)}, u32[]{:S(2)}, u32[]{:S(2)}) %collective-permute-start.5) | collective-permute-done | bytes 73760 | tf_op jit(solution)/shard_map/ppermute | solution.py:438
  20.6 0.0 collective-permute-done.4.ca_ref
  20.6 0.0 copy-done.2
  20.6 0.6 %copy-done.3 = f32[72,256]{1,0:T(8,128)} copy-done((f32[72,256]{1,0:T(8,128)}, f32[72,256]{1,0:T(8,128)S(1)}, u32[]{:S(2)}) %copy-start.3) | copy-done | bytes 73752
  21.2 0.6 %copy-done.4 = f32[72,256]{1,0:T(8,128)} copy-done((f32[72,256]{1,0:T(8,128)}, f32[72,256]{1,0:T(8,128)S(1)}, u32[]{:S(2)}) %copy-start.4) | copy-done | bytes 73752
  21.9 2.8 %unpack.1 = (f32[4,24,32,128]{3,2,1,0:T(8,128)}, f32[24,32,128]{2,1,0:T(8,128)}, f32[2,32,128]{2,1,0:T(8,128)}) custom-call(s32[4]{0:T(128)} %pad_add_fusion.where_ref, f32[72,256]{1,0:T(8,128)} %copy-done.2, f32[72,256]{1,0:T(8,128)} %copy-done.4, f32[72,256]{1,0:T(8,128)} %copy-done.3), custom_call_target="tpu_custom_call" | custom-call | tf_op jit(solution)/shard_map/unpack/pallas_call | solution.py:442
  24.6 0.0 collective-permute-done.xa_ref
  24.6 0.0 collective-permute-done.1.xb_ref
  24.7 0.0 copy-start.1
  24.7 0.7 %copy-done = f32[26,32,128]{2,1,0:T(8,128)} copy-done((f32[26,32,128]{2,1,0:T(8,128)}, f32[26,32,128]{2,1,0:T(8,128)S(1)}, u32[]{:S(2)}) %copy-start) | copy-done | bytes 426008
  25.4 0.1 copy-done.1
  25.6 12.4 %sweeps.1 = (f32[8,32,128]{2,1,0:T(8,128)}, f32[8,32,128]{2,1,0:T(8,128)}, f32[3,8,32,128]{3,2,1,0:T(8,128)}) custom-call(s32[4]{0:T(128)} %pad_add_fusion.where_ref, s32[8,32,128]{2,1,0:T(8,128)} %ph_ref.3, f32[8,32,128]{2,1,0:T(8,128)} %dv_ref.3, f32[8,32,128]{2,1,0:T(8,128)} %p_ref.3, f32[3,8,32,128]{3,2,1,0:T(8,128)} %vc_ref.3, ...), custom_call_target="tpu_custom_call" | custom-call | tf_op jit(solution)/shard_map/sweeps/pallas_call | solution.py:452
  (5 shorter events, 0.0 us)
Async XLA Ops:
  3.9 4.2 %collective-permute-start.2 = (f32[32,256]{1,0:T(8,128)}, f32[32,256]{1,0:T(8,128)S(1)}, u32[]{:S(2)}, u32[]{:S(2)}) collective-permute-start(f32[32,256]{1,0:T(8,128)} %get-tuple-element.15), channel_id=1, source_target_pairs={{0,1},{4,5},{8,9},{12,13},{16,17},{20,21},{24,25},{28,29},{1,0},{5... | collective-permute-start | bytes 98312 | tf_op jit(solution)/shard_map/ppermute | solution.py:435
  6.0 18.6 %collective-permute-start = (f32[26,32,128]{2,1,0:T(8,128)}, f32[26,32,128]{2,1,0:T(8,128)S(1)}, u32[]{:S(2)}, u32[]{:S(2)}) collective-permute-start(f32[26,32,128]{2,1,0:T(8,128)} %get-tuple-element.13), channel_id=1, source_target_pairs={{0,4},{1,5},{2,6},{3,7},{4,0},{5,1},{6,2},{7,3},{8,12},{9,13},{10,... | collective-permute-start | bytes 1277960 | tf_op jit(solution)/shard_map/ppermute | solution.py:434
  7.0 17.7 %collective-permute-start.1 = (f32[26,32,128]{2,1,0:T(8,128)}, f32[26,32,128]{2,1,0:T(8,128)S(1)}, u32[]{:S(2)}, u32[]{:S(2)}) collective-permute-start(f32[26,32,128]{2,1,0:T(8,128)} %get-tuple-element.14), channel_id=1, source_target_pairs={{0,1},{1,0},{2,3},{3,2},{4,8},{5,9},{6,10},{7,11},{8,4},{9,5},{10,... | collective-permute-start | bytes 1277960 | tf_op jit(solution)/shard_map/ppermute | solution.py:433
  8.1 1.4 %collective-permute-start.3 = (f32[32,256]{1,0:T(8,128)}, f32[32,256]{1,0:T(8,128)S(1)}, u32[]{:S(2)}, u32[]{:S(2)}) collective-permute-start(f32[32,256]{1,0:T(8,128)} %get-tuple-element.16), channel_id=1, source_target_pairs={{0,4},{4,0},{8,12},{12,8},{16,20},{20,16},{24,28},{28,24},{1,2},{5... | collective-permute-start | bytes 98312 | tf_op jit(solution)/shard_map/ppermute | solution.py:436
  10.2 10.4 %copy-start.2 = (f32[72,256]{1,0:T(8,128)}, f32[72,256]{1,0:T(8,128)S(1)}, u32[]{:S(2)}) copy-start(f32[72,256]{1,0:T(8,128)S(1)} %constant_dynamic-update-slice_fusion.own_ref) | copy-start | bytes 221188
  10.2 10.4 %collective-permute-start.5 = (f32[72,256]{1,0:T(8,128)S(1)}, f32[72,256]{1,0:T(8,128)S(1)}, u32[]{:S(2)}, u32[]{:S(2)}) collective-permute-start(f32[72,256]{1,0:T(8,128)S(1)} %constant_dynamic-update-slice_fusion.own_ref), channel_id=1, source_target_pairs={{0,1},{1,0},{2,3},{3,2},{4,8},{5,9},{6,10},{7,11},{8,4},{9,5},{10,... | collective-permute-start | bytes 221192 | tf_op jit(solution)/shard_map/ppermute | solution.py:438
  11.5 9.2 %collective-permute-start.4 = (f32[72,256]{1,0:T(8,128)S(1)}, f32[72,256]{1,0:T(8,128)S(1)}, u32[]{:S(2)}, u32[]{:S(2)}) collective-permute-start(f32[72,256]{1,0:T(8,128)S(1)} %constant_dynamic-update-slice_fusion.own_ref), channel_id=1, source_target_pairs={{0,4},{1,5},{2,6},{3,7},{4,0},{5,1},{6,2},{7,3},{8,12},{9,13},{10,... | collective-permute-start | bytes 221192 | tf_op jit(solution)/shard_map/ppermute | solution.py:439
  20.6 0.6 %copy-start.3 = (f32[72,256]{1,0:T(8,128)}, f32[72,256]{1,0:T(8,128)S(1)}, u32[]{:S(2)}) copy-start(f32[72,256]{1,0:T(8,128)S(1)} %collective-permute-done.5.cb_ref) | copy-start | bytes 221188
  21.2 0.6 %copy-start.4 = (f32[72,256]{1,0:T(8,128)}, f32[72,256]{1,0:T(8,128)S(1)}, u32[]{:S(2)}) copy-start(f32[72,256]{1,0:T(8,128)S(1)} %collective-permute-done.4.ca_ref) | copy-start | bytes 221188
  24.6 0.8 %copy-start = (f32[26,32,128]{2,1,0:T(8,128)}, f32[26,32,128]{2,1,0:T(8,128)S(1)}, u32[]{:S(2)}) copy-start(f32[26,32,128]{2,1,0:T(8,128)S(1)} %collective-permute-done.xa_ref) | copy-start | bytes 1277956
  24.7 0.9 %copy-start.1 = (f32[26,32,128]{2,1,0:T(8,128)}, f32[26,32,128]{2,1,0:T(8,128)S(1)}, u32[]{:S(2)}) copy-start(f32[26,32,128]{2,1,0:T(8,128)S(1)} %collective-permute-done.1.xb_ref) | copy-start | bytes 1277956

commit v2 on v0

v2 whole, which is shorter than its diff:
```python
import math

import jax
import jax.numpy as jnp
from jax import lax
from jax.experimental import pallas as pl
from jax.experimental.pallas import tpu as pltpu
from jax.sharding import PartitionSpec as P

SWEEPS = 6

gas_density = 0.25
lower_bound = 0.25
upper_bound = 2.0

FACE = (1.0, 2.0 / (1.0 + gas_density), 1.0 / gas_density)


def chebyshev_weights(count):
    center = 0.5 * (upper_bound + lower_bound)
    radius = 0.5 * (upper_bound - lower_bound)
    roots = [
        center + radius * math.cos(math.pi * (2 * number + 1) / (2 * count))
        for number in range(count)
    ]
    order = []
    for number in range(count // 2):
        order.append(number)
        order.append(count - 1 - number)
    return [1.0 / roots[position] for position in order]


def face(pair):
    return jnp.where(pair < 0.5, FACE[0], jnp.where(pair < 1.5, FACE[1], FACE[2]))


def iota(dim):
    return lax.broadcasted_iota(jnp.int32, (32, 128), dim)


def y_up(v):
    return pltpu.roll(v, v.shape[0] - 1, 0)


def y_down(v):
    return pltpu.roll(v, 1, 0)


def z_up(v):
    return pltpu.roll(v, v.shape[1] - 1, 1)


def z_down(v):
    return pltpu.roll(v, 1, 1)


HALO = SWEEPS + 1
ROWS = 32
SCOPED = 16 * 2**20


def pack_kernel(ph_ref, dv_ref, p_ref, vc_ref, xa_ref, xb_ref, za_ref, zb_ref, row_ref, adj_ref, up_ref, down_ref):
    cells_x = ph_ref.shape[0]
    x_even = lax.axis_index("wide") % 2 == 0
    z_even = lax.axis_index("narrow") % 2 == 0
    lane = iota(1)
    row = iota(0)
    before = None
    for i in range(cells_x):
        ph = ph_ref[i].astype(jnp.float32)
        adj = jnp.zeros_like(ph)
        if before is not None:
            adj = adj - before
        if i + 1 < cells_x:
            before = face(ph + ph_ref[i + 1].astype(jnp.float32)) * vc_ref[0, i]
            adj = adj + before
        flux = face(ph + jnp.where(row == ph.shape[0] - 1, ph, y_up(ph))) * vc_ref[1, i]
        adj = adj + flux - jnp.where(row == 0, 0.0, y_down(flux))
        flux = jnp.where(lane == ph.shape[1] - 1, 0.0, face(ph + z_up(ph)) * vc_ref[2, i])
        adj = adj + flux - z_down(flux)
        adj_ref[i] = adj

    first = cells_x - HALO
    n = SWEEPS

    def upward(out):
        out[0:HALO] = ph_ref[first:].astype(jnp.float32)
        out[HALO : HALO + n] = dv_ref[first + 1 :]
        out[HALO + n : HALO + 2 * n] = adj_ref[first + 1 :]
        out[HALO + 2 * n : HALO + 3 * n] = p_ref[first + 1 :]
        out[HALO + 3 * n] = vc_ref[0, cells_x - 1]

    def downward(out):
        out[0:HALO] = ph_ref[0:HALO].astype(jnp.float32)
        out[HALO : HALO + n] = dv_ref[0:n]
        out[HALO + n : HALO + 2 * n] = adj_ref[0:n]
        out[HALO + 2 * n : 2 * HALO + 2 * n] = p_ref[0:HALO]

    @pl.when(x_even)
    def _():
        upward(xa_ref)
        downward(xb_ref)

    @pl.when(jnp.logical_not(x_even))
    def _():
        upward(xb_ref)
        downward(xa_ref)

    cells = cells_x * ph_ref.shape[1]
    width = ph_ref.shape[2]

    def turned(v):
        return v.reshape(cells, width).T

    t = turned(ph_ref[...].astype(jnp.float32))
    up_ref[0:HALO] = t[width - HALO :]
    down_ref[0:HALO] = t[0:HALO]
    t = turned(dv_ref[...])
    up_ref[HALO : HALO + n] = t[width - n :]
    down_ref[HALO : HALO + n] = t[0:n]
    t = turned(adj_ref[...])
    up_ref[HALO + n : HALO + 2 * n] = t[width - n :]
    down_ref[HALO + n : HALO + 2 * n] = t[0:n]
    t = turned(p_ref[...])
    up_ref[HALO + 2 * n : HALO + 3 * n] = t[width - n :]
    down_ref[HALO + 2 * n : 2 * HALO + 2 * n] = t[0:HALO]
    t = turned(vc_ref[2])
    up_ref[HALO + 3 * n : HALO + 3 * n + 1] = t[width - 1 :]
    row_ref[...] = t[width - 8 :]
    t = turned(vc_ref[0])
    up_ref[2 * HALO + 2 * n + 0 : 2 * HALO + 3 * n] = t[width - n :]
    down_ref[2 * HALO + 2 * n : 2 * HALO + 3 * n] = t[0:n]

    @pl.when(z_even)
    def _():
        za_ref[...] = up_ref[...]
        zb_ref[...] = down_ref[...]

    @pl.when(jnp.logical_not(z_even))
    def _():
        zb_ref[...] = up_ref[...]
        za_ref[...] = down_ref[...]


def join_kernel(za_ref, zb_ref, edge_ref, out_ref):
    out_ref[0:ROWS] = za_ref[...]
    out_ref[ROWS : 2 * ROWS] = zb_ref[...]
    out_ref[2 * ROWS :] = edge_ref[...]


class Local:
    def __init__(self, shape, h, e, f0, c, s, ps, us, diag, vx):
        self.cells_x, self.ny, self.width = shape
        self.planes = 3 * self.cells_x
        self.h, self.e, self.f0, self.c, self.s, self.ps, self.us, self.diag, self.vx = h, e, f0, c, s, ps, us, diag, vx
        wi, ni = lax.axis_index("wide"), lax.axis_index("narrow")
        self.x_even, self.z_even = wi % 2 == 0, ni % 2 == 0
        self.x_first, self.x_last = wi == 0, wi == lax.axis_size("wide") - 1
        self.z_first, self.z_last = ni == 0, ni == lax.axis_size("narrow") - 1
        lane, self.row = iota(1), iota(0)
        self.lane0, self.lane_end = lane == 0, lane == self.width - 1
        side_high = jnp.logical_and(lane <= HALO - 1, jnp.logical_not(self.z_last))
        side_low = jnp.logical_and(lane >= self.width - HALO, jnp.logical_not(self.z_first))
        self.side = jnp.logical_or(side_low, side_high)
        self.core = jnp.logical_and(self.side, jnp.logical_or(lane < HALO - 1, lane > self.width - HALO))

    def at(self, lead, i):
        return pl.ds((lead * self.planes + i + self.cells_x) * self.ny, self.ny)

    def shifted(self, lead, i, by):
        return pl.ds((lead * self.planes + i + self.cells_x) * self.ny + by, self.ny)

    def masked(self, i, col, value, cover):
        flag = None
        if i < 0:
            flag = jnp.logical_not(self.x_first)
        elif i >= self.cells_x:
            flag = jnp.logical_not(self.x_last)
        if col == 0:
            return value if flag is None else jnp.where(flag, value, 0.0)
        return jnp.where(cover if flag is None else jnp.logical_and(cover, flag), value, 0.0)

    def halo_columns(self, part, t_ref, first):
        n, width, ny, cells_x = SWEEPS, self.width, self.ny, self.cells_x
        zl = jnp.where(self.z_even, part[ROWS : 2 * ROWS], part[0:ROWS])
        zh = jnp.where(self.z_even, part[0:ROWS], part[ROWS : 2 * ROWS])
        t_ref[0, 0:HALO] = zh[0:HALO]
        t_ref[0, width - HALO :] = zl[0:HALO]
        for field in (1, 2):
            start = HALO + (field - 1) * n
            t_ref[field, 0:n] = zh[start : start + n]
            t_ref[field, width - n :] = zl[start : start + n]
        start = HALO + 2 * n
        t_ref[3, 0:HALO] = zh[start : start + HALO]
        t_ref[3, width - n :] = zl[start : start + n]
        below = jnp.where(self.z_first, 0.0, zl[start + n : start + n + 1])
        above = part[2 * ROWS + 7 : 2 * ROWS + 8]
        t_ref[4, width - 1 :] = below
        t_ref[4, 0:1] = above
        t_ref[5, width - 1 :] = above
        t_ref[5, 0:1] = below
        for field in range(6):
            self.h[pl.ds((field * self.planes + first + cells_x) * ny, cells_x * ny)] = t_ref[field].T
        if first == cells_x:
            return
        last = slice((cells_x - 1) * ny, cells_x * ny)
        t_ref[0, 0:n, 0:ny] = zh[2 * HALO + 2 * n :, last]
        t_ref[0, width - n :, 0:ny] = zl[2 * HALO + 2 * n :, last]
        number = 0 if first < 0 else 1
        self.vx[pl.ds(number * ny, ny)] = t_ref[0, :, 0:128].T[0:ny]

    def phases(self, i, value):
        self.e[self.at(0, i)] = value
        low = jnp.logical_and(self.lane_end, self.z_first)
        high = jnp.logical_and(self.lane0, self.z_last)
        other = self.h[self.at(0, i)]
        self.e[self.at(1, i)] = jnp.where(high, z_down(value), jnp.where(low, z_up(value), other))

    def start(self, i, value):
        self.ps[self.at(0, i)] = self.masked(i, 0, value, None)
        self.ps[self.at(1, i)] = self.masked(i, 1, self.h[self.at(3, i)], self.side)

    def faces_x(self, i):
        for col in range(2):
            self.f0[self.at(col, i)] = face(self.e[self.at(col, i)] + self.e[self.at(col, i + 1)])

    def setup(self, i, source, adj, cross):
        ny, row = self.ny, self.row
        ph = [self.e[self.at(col, i)] for col in range(2)]
        up_z = [z_up(v) for v in ph]
        f2 = [face(ph[col] + jnp.where(self.lane_end, up_z[1 - col], up_z[col])) for col in range(2)]
        down_z = [z_down(v) for v in f2]
        for col in range(2):
            l2 = jnp.where(self.lane0, down_z[1 - col], down_z[col])
            up = self.e[self.shifted(col, i, 1)]
            down = self.e[self.shifted(col, i, -1)]
            f1 = face(ph[col] + jnp.where(row == ny - 1, ph[col], up))
            l1 = face(ph[col] + jnp.where(row == 0, ph[col], down))
            f0 = self.f0[self.at(col, i)]
            l0 = self.f0[self.at(col, i - 1)]
            diag = f0 + l0 + f1 + l1 + f2[col] + l2
            inv = self.masked(i, col, 1.0 / diag, self.core)
            if col == 0 and 0 <= i < self.cells_x:
                self.diag[pl.ds(i * ny, ny)] = diag
            for number, value in enumerate((f0, l0, jnp.where(row == ny - 1, 0.0, f1), jnp.where(row == 0, 0.0, l1), f2[col], l2)):
                self.c[self.at(2 * number + col, i)] = value * inv
            value = adj if col == 0 else self.h[self.at(2, i)]
            right = source if col == 0 else self.h[self.at(1, i)]
            if i in cross:
                value = value + cross[i][col]
            if i - 1 in cross:
                value = value - cross[i - 1][col]
            value = value + jnp.where(self.lane0, -l2, f2[col]) * self.h[self.at(5 - col, i)]
            if col == 1:
                value = jnp.where(self.core, value, 0.0)
                right = jnp.where(self.core, right, 0.0)
            self.s[self.at(col, i)] = right * inv
            self.us[self.at(col, i)] = value * inv

    def spread(self, state, k, i):
        v = [state[self.at(2 * k + col, i)] for col in range(2)]
        up_z = [z_up(x) for x in v]
        down_z = [z_down(x) for x in v]
        out = []
        for col in range(2):
            lead = 2 * k + col
            up = jnp.where(self.lane_end, up_z[1 - col], up_z[col])
            down = jnp.where(self.lane0, down_z[1 - col], down_z[col])
            total = self.c[self.at(col, i)] * state[self.at(lead, i + 1)] + self.c[self.at(2 + col, i)] * state[self.at(lead, i - 1)]
            total = total + self.c[self.at(4 + col, i)] * state[self.shifted(lead, i, 1)]
            total = total + self.c[self.at(6 + col, i)] * state[self.shifted(lead, i, -1)]
            out.append(total + self.c[self.at(8 + col, i)] * up + self.c[self.at(10 + col, i)] * down)
        return v, out

    def sweep_p(self, k, i):
        w = chebyshev_weights(SWEEPS)[k]
        v, total = self.spread(self.ps, k, i)
        for col in range(2):
            self.ps[self.at(2 * k + 2 + col, i)] = (1.0 - w) * v[col] + w * (self.s[self.at(col, i)] + total[col])

    def sweep_u(self, k, i):
        w = chebyshev_weights(SWEEPS)[SWEEPS - 1 - k]
        v, total = self.spread(self.us, k, i)
        for col in range(2):
            self.us[self.at(2 * k + 2 + col, i)] = (1.0 - w) * v[col] + w * total[col]


def early(k, cells_x):
    return range(1 + k, cells_x - 1 - k), range(2 + k, cells_x - 2 - k)


def own_kernel(
    ph_ref, dv_ref, p_ref, adj_ref, own_ref,
    h_ref, e_ref, f0_ref, c_ref, s_ref, ps_ref, us_ref, diag_ref, vx_ref, t_ref,
):
    g = Local(ph_ref.shape, h_ref, e_ref, f0_ref, c_ref, s_ref, ps_ref, us_ref, diag_ref, vx_ref)
    cells_x = g.cells_x
    t_ref[...] = jnp.zeros_like(t_ref)
    g.halo_columns(own_ref[...], t_ref, 0)
    for i in range(cells_x):
        g.phases(i, ph_ref[i].astype(jnp.float32))
        g.start(i, p_ref[i])
    zero = jnp.zeros((g.ny, g.width), jnp.float32)
    for col in range(2):
        for i in (-1, cells_x):
            e_ref[g.at(col, i)] = zero
            for k in range(SWEEPS):
                for state in (ps_ref, us_ref):
                    state[g.at(2 * k + col, i)] = zero
        for k in range(SWEEPS):
            for i in range(cells_x):
                if k > 0 and i not in early(k - 1, cells_x)[0]:
                    ps_ref[g.at(2 * k + col, i)] = zero
                us_ref[g.at(2 * k + col, i)] = zero
    for i in range(cells_x - 1):
        g.faces_x(i)
    for i in range(1, cells_x - 1):
        g.setup(i, dv_ref[i], adj_ref[i], {})
    for k in range(SWEEPS):
        for_p, for_u = early(k, cells_x)
        for i in for_p:
            g.sweep_p(k, i)
        for i in for_u:
            g.sweep_u(k, i)


def main_kernel(
    ph_ref, dv_ref, p_ref, vc_ref, adj_ref, xa_ref, xb_ref, ca_ref, cb_ref,
    h_in, e_in, f0_in, c_in, s_in, ps_in, us_in, diag_in, vx_in,
    h_ref, e_ref, f0_ref, c_ref, s_ref, ps_ref, us_ref, diag_ref, vx_ref, gd_ref, gp_ref, gf_ref,
    t_ref, r_ref,
):
    g = Local(ph_ref.shape, h_ref, e_ref, f0_ref, c_ref, s_ref, ps_ref, us_ref, diag_ref, vx_ref)
    cells_x, ny, width, row = g.cells_x, g.ny, g.width, g.row
    n = SWEEPS
    weights = chebyshev_weights(SWEEPS)
    lane_end = g.lane_end

    def low(k):
        return jnp.where(g.x_even, xb_ref[k], xa_ref[k])

    def high(k):
        return jnp.where(g.x_even, xa_ref[k], xb_ref[k])

    t_ref[...] = jnp.zeros_like(t_ref)
    g.halo_columns(jnp.where(g.x_even, cb_ref[...], ca_ref[...]), t_ref.at[0], -cells_x)
    g.halo_columns(jnp.where(g.x_even, ca_ref[...], cb_ref[...]), t_ref.at[1], cells_x)
    for k in range(HALO):
        g.phases(k - HALO, low(k))
        g.phases(cells_x + k, high(k))
    for col in range(2):
        e_ref[g.at(col, -1)] = jnp.where(g.x_first, e_ref[g.at(col, 0)], e_ref[g.at(col, -1)])
        end = e_ref[g.at(col, cells_x - 1)]
        e_ref[g.at(col, cells_x)] = jnp.where(g.x_last, end, e_ref[g.at(col, cells_x)])
    for i in range(-n, 0):
        g.start(i, low(HALO + 3 * n + i))
    for i in range(cells_x, cells_x + HALO):
        g.start(i, high(HALO + 2 * n + i - cells_x))
    for i in (*range(-HALO, 0), *range(cells_x - 1, cells_x + n)):
        g.faces_x(i)

    cross = {}
    for number, i in enumerate((-1, cells_x - 1)):
        value = low(HALO + 3 * n) if i < 0 else vc_ref[0, i]
        flux = (f0_ref[g.at(0, i)] * value, f0_ref[g.at(1, i)] * vx_ref[pl.ds(number * ny, ny)])
        cross[i] = tuple(jnp.where(g.x_first, 0.0, v) for v in flux) if i < 0 else flux

    zero = jnp.zeros((ny, width), jnp.float32)
    for col in range(2):
        for i in (-n - 1, cells_x + n):
            us_ref[g.at(col, i)] = zero
    for i in (*range(-n, 1), *range(cells_x - 1, cells_x + n)):
        if i < 0:
            g.setup(i, low(HALO + n + i), low(HALO + 2 * n + i), cross)
        elif i >= cells_x:
            g.setup(i, high(HALO + i - cells_x), high(HALO + n + i - cells_x), cross)
        else:
            g.setup(i, dv_ref[i], adj_ref[i], cross)

    for k in range(n):
        for_p, for_u = early(k, cells_x)
        for i in range(-(n - 1) + k, cells_x + n - k):
            if i not in for_p:
                g.sweep_p(k, i)
            if i not in for_u and i < cells_x + n - 1 - k:
                g.sweep_u(k, i)

    for i in range(cells_x + 1):
        for col in range(2):
            total = None
            for k in range(n):
                term = us_ref[g.at(2 * (n - 1 - k) + col, i)] * (ps_ref[g.at(2 * k + 2 + col, i)] - ps_ref[g.at(2 * k + col, i)])
                total = term if total is None else total + term
            r_ref[g.at(col, i)] = total

    def rises(state, k, i):
        v = state[g.at(2 * k, i)]
        z_next = jnp.where(lane_end, z_up(state[g.at(2 * k + 1, i)]), z_up(v))
        y_next = jnp.where(row == ny - 1, 0.0, state[g.shifted(2 * k, i, 1)])
        return v, (state[g.at(2 * k, i + 1)] - v, y_next - v, z_next - v)

    for i in range(cells_x):
        gp_ref[i] = us_ref[g.at(2 * n, i)] * diag_ref[pl.ds(i * ny, ny)]
        gd = zero
        terms = [zero] * 3
        for k in range(n):
            u, rise_u = rises(us_ref, n - 1 - k, i)
            _, rise_p = rises(ps_ref, k, i)
            gd = gd + weights[k] * u
            for a in range(3):
                terms[a] = terms[a] + weights[k] * (rise_u[a] * rise_p[a])
        gd_ref[i] = gd
        _, rise = rises(ps_ref, n, i)
        r = r_ref[g.at(0, i)]
        y_next = jnp.where(row == ny - 1, 0.0, r_ref[g.shifted(0, i, 1)])
        z_next = jnp.where(lane_end, z_up(r_ref[g.at(1, i)]), z_up(r))
        nexts = (r_ref[g.at(0, i + 1)], y_next, z_next)
        for a in range(3):
            gf_ref[a, i] = -vc_ref[a, i] * rise[a] - terms[a] - (r + nexts[a])


def swaps(size, other, odd, spare_first):
    pairs = []
    for i in range(size):
        for k in range(other):
            partner = ((i + 1) ^ 1) - 1 if odd else i ^ 1
            target = (partner, k) if 0 <= partner < size else (i, k ^ 1)
            source = (i, k)
            pairs.append((source, target))
    return pairs


def flat_pairs(pairs, narrow, turned):
    def flat(at):
        return at[1] * narrow + at[0] if turned else at[0] * narrow + at[1]

    return [(flat(source), flat(target)) for source, target in pairs]


def per_device(divergence, pressure_start, phase, velocity_cot):
    cells_x, ny, cells_z = divergence.shape
    wide, narrow = lax.axis_size("wide"), lax.axis_size("narrow")
    axes = ("wide", "narrow")
    x_even = flat_pairs(swaps(wide, narrow, False, True), narrow, False)
    x_odd = flat_pairs(swaps(wide, narrow, True, True), narrow, False)
    z_even = flat_pairs(swaps(narrow, wide, False, True), narrow, True)
    z_odd = flat_pairs(swaps(narrow, wide, True, True), narrow, True)
    f32 = jnp.float32
    vmem = pl.BlockSpec(memory_space=pltpu.VMEM)

    def kept(*dims):
        return pltpu.VMEM(dims, f32)

    def near(v):
        return pltpu.with_memory_space_constraint(v, pltpu.VMEM)

    slots = 2 * HALO + 2 * SWEEPS
    cells = cells_x * ny
    phase, divergence, pressure_start, velocity_cot = (
        near(v) for v in (phase, divergence, pressure_start, velocity_cot)
    )
    xa, xb, za, zb, edge, adj = pl.pallas_call(
        pack_kernel,
        out_shape=(
            kept(slots, ny, cells_z), kept(slots, ny, cells_z), kept(ROWS, cells), kept(ROWS, cells),
            kept(8, cells), kept(cells_x, ny, cells_z),
        ),
        in_specs=[vmem] * 4,
        out_specs=(vmem,) * 6,
        scratch_shapes=[pltpu.VMEM((ROWS, cells), f32)] * 2,
        compiler_params=pltpu.CompilerParams(vmem_limit_bytes=SCOPED),
        name="pack",
    )(phase, divergence, pressure_start, velocity_cot)

    got_xb = near(lax.ppermute(xb, axes, x_odd))
    got_xa = near(lax.ppermute(xa, axes, x_even))
    got_za = near(lax.ppermute(za, axes, z_even))
    got_zb = near(lax.ppermute(zb, axes, z_odd))
    corner = pl.pallas_call(
        join_kernel,
        out_shape=kept(2 * ROWS + 8, cells),
        in_specs=[vmem] * 3,
        out_specs=vmem,
        compiler_params=pltpu.CompilerParams(vmem_limit_bytes=SCOPED),
        name="join",
    )(got_za, got_zb, edge)
    got_cb = near(lax.ppermute(corner, axes, x_odd))
    got_ca = near(lax.ppermute(corner, axes, x_even))

    rows = 3 * cells_x * ny
    layers = (6, 2, 2, 12, 2, 2 * (SWEEPS + 1), 2 * (SWEEPS + 1))
    shapes = (*(kept(layer * rows, cells_z) for layer in layers), kept(cells_x * ny, cells_z), kept(2 * ny, cells_z))
    state = pl.pallas_call(
        own_kernel,
        out_shape=shapes,
        in_specs=[vmem] * 5,
        out_specs=(vmem,) * len(shapes),
        scratch_shapes=[pltpu.VMEM((6, cells_z, cells), f32)],
        compiler_params=pltpu.CompilerParams(vmem_limit_bytes=SCOPED),
        name="own",
    )(phase, divergence, pressure_start, adj, corner)

    block = jax.ShapeDtypeStruct((cells_x, ny, cells_z), f32)
    out = pl.pallas_call(
        main_kernel,
        out_shape=(*shapes, block, block, jax.ShapeDtypeStruct((3, cells_x, ny, cells_z), f32)),
        in_specs=[vmem] * (9 + len(shapes)),
        out_specs=(vmem,) * (len(shapes) + 3),
        input_output_aliases={9 + number: number for number in range(len(shapes))},
        scratch_shapes=[pltpu.VMEM((2, 6, cells_z, cells), f32), pltpu.VMEM((2 * rows, cells_z), f32)],
        compiler_params=pltpu.CompilerParams(vmem_limit_bytes=SCOPED),
        name="sweeps",
    )(phase, divergence, pressure_start, velocity_cot, adj, got_xa, got_xb, got_ca, got_cb, *state)
    return out[-3:]


def solution(mesh):
    in_specs = (
        P("wide", None, "narrow"),
        P("wide", None, "narrow"),
        P("wide", None, "narrow"),
        P(None, "wide", None, "narrow"),
    )
    out_specs = (
        P("wide", None, "narrow"),
        P("wide", None, "narrow"),
        P(None, "wide", None, "narrow"),
    )
    return jax.shard_map(
        per_device, mesh=mesh, in_specs=in_specs, out_specs=out_specs, check_vma=False
    )
```

time: 141 us -> 28.9 us (0.20)
  the two profiles are of different devices: /device:TPU:28 before, /device:TPU:1 now
where the time goes in v2:
time: 28.9 us; the launch traced here: 28.7 us
  starting transfers between devices  9.99 us (35%)
  Pallas kernels  9.33 us (32%)
  local copies, waits for them, and re-layouts  6.5 us (22%)
  waiting for transfers between devices  2.12 us (7%)
  between operations  0.71 us (2%)
    pallas_call x1, Pallas kernels, per_device(): pl.pallas_call(main_kernel, out_shape=(*shapes, block, block, jax.ShapeDt...  7.43 us
    unnamed x14, local copies, waits for them, and re-layouts  6.5 us
    ppermute x1, starting transfers between devices, per_device(): got_ca = near(lax.ppermute(corner, axes, x_even))  5.27 us
    ppermute x1, starting transfers between devices, per_device(): got_xb = near(lax.ppermute(xb, axes, x_odd))  2.65 us
    ppermute x1, waiting for transfers between devices, per_device(): got_za = near(lax.ppermute(za, axes, z_even))  2.11 us
    pallas_call x1, Pallas kernels, per_device(): pl.pallas_call(own_kernel, out_shape=shapes, in_specs=[vmem] * 5, out_spe...  1.39 us
    ppermute x1, starting transfers between devices, per_device(): got_za = near(lax.ppermute(za, axes, z_even))  1.3 us
    ppermute x1, starting transfers between devices, per_device(): got_cb = near(lax.ppermute(corner, axes, x_odd))  0.7 us
  transfers between devices with their start and end apart: 6, of which 1 were waited for; matrix products, arithmetic and copies ran while one was open for 0% of the time, Pallas kernels for 5%

profile of v2, /device:TPU:1, one launch (start us, length us, event | category | flops | bytes accessed | tf_op | source)
XLA Modules:
  0.0 28.7 jit_solution(3753352038423518322)
XLA Ops:
  0.6 0.0 copy-start
  0.6 1.0 %copy-done = f32[3,8,32,128]{3,2,1,0:T(8,128)S(1)} copy-done((f32[3,8,32,128]{3,2,1,0:T(8,128)S(1)}, f32[3,8,32,128]{3,2,1,0:T(8,128)}, u32[]{:S(2)}) %copy-start) | copy-done | bytes 393240
  1.6 0.9 %copy-done.2 = s32[8,32,128]{2,1,0:T(8,128)S(1)} copy-done((s32[8,32,128]{2,1,0:T(8,128)S(1)}, s32[8,32,128]{2,1,0:T(8,128)}, u32[]{:S(2)}) %copy-start.2) | copy-done | bytes 131096
  2.5 0.9 %copy-done.4 = f32[8,32,128]{2,1,0:T(8,128)S(1)} copy-done((f32[8,32,128]{2,1,0:T(8,128)S(1)}, f32[8,32,128]{2,1,0:T(8,128)}, u32[]{:S(2)}) %copy-start.4) | copy-done | bytes 131096
  3.4 0.9 %copy-done.6 = f32[8,32,128]{2,1,0:T(8,128)S(1)} copy-done((f32[8,32,128]{2,1,0:T(8,128)S(1)}, f32[8,32,128]{2,1,0:T(8,128)}, u32[]{:S(2)}) %copy-start.6) | copy-done | bytes 131096
  4.3 0.5 %pack.1 = (f32[26,32,128]{2,1,0:T(8,128)S(1)}, f32[26,32,128]{2,1,0:T(8,128)S(1)}, f32[32,256]{1,0:T(8,128)S(1)}, f32[32,256]{1,0:T(8,128)S(1)}, f32[8,256]{1,0:T(8,128)S(1)}, /*index=5*/f32[8,32,128]{2,1,0:T(8,128)S(1)}) custom-call(s32[8,32,128]{2,1,0:T(8,128)S(1)} %copy-done.2, f32[8,32,128]{2,1,0:T(8,128)S(1)} %copy-done.4, f32[8,32,128]{2,1,0:T(8,128)S(1)} %copy-done.6, ...), custom_call_target="tpu_custom_call" | custom-call | tf_op jit(solution)/shard_map/pack/pallas_call | solution.py:462
  4.9 0.1 collective-permute-start
  4.9 2.6 %collective-permute-start.1 = (f32[26,32,128]{2,1,0:T(8,128)S(1)}, f32[26,32,128]{2,1,0:T(8,128)S(1)}, u32[]{:S(2)}, u32[]{:S(2)}) collective-permute-start(f32[26,32,128]{2,1,0:T(8,128)S(1)} %get-tuple-element.23), channel_id=1, source_target_pairs={{0,1},{1,0},{2,3},{3,2},{4,8},{5,9},{6,10},{7,11},{8,4},{9,5},{10,... | collective-permute-start | bytes 1277960 | tf_op jit(solution)/shard_map/ppermute | solution.py:475
  7.6 1.3 %collective-permute-start.2 = (f32[32,256]{1,0:T(8,128)S(1)}, f32[32,256]{1,0:T(8,128)S(1)}, u32[]{:S(2)}, u32[]{:S(2)}) collective-permute-start(f32[32,256]{1,0:T(8,128)S(1)} %get-tuple-element.24), channel_id=1, source_target_pairs={{0,1},{4,5},{8,9},{12,13},{16,17},{20,21},{24,25},{28,29},{1,0},{5... | collective-permute-start | bytes 98312 | tf_op jit(solution)/shard_map/ppermute | solution.py:477
  8.9 0.0 collective-permute-start.3
  8.9 2.1 %collective-permute-done.2.za_ref = f32[32,256]{1,0:T(8,128)S(1)} collective-permute-done((f32[32,256]{1,0:T(8,128)S(1)}, f32[32,256]{1,0:T(8,128)S(1)}, u32[]{:S(2)}, u32[]{:S(2)}) %collective-permute-start.2) | collective-permute-done | bytes 32800 | tf_op jit(solution)/shard_map/ppermute | solution.py:477
  11.0 0.0 collective-permute-done.3.zb_ref
  11.0 0.7 %collective-permute-start.5 = (f32[72,256]{1,0:T(8,128)S(1)}, f32[72,256]{1,0:T(8,128)S(1)}, u32[]{:S(2)}, u32[]{:S(2)}) collective-permute-start(f32[72,256]{1,0:T(8,128)S(1)} %join.1.own_ref), channel_id=1, source_target_pairs={{0,1},{1,0},{2,3},{3,2},{4,8},{5,9},{6,10},{7,11},{8,4},{9,5},{10,... | collective-permute-start | bytes 221192 | tf_op jit(solution)/shard_map/ppermute | solution.py:487
  11.7 5.3 %collective-permute-start.4 = (f32[72,256]{1,0:T(8,128)S(1)}, f32[72,256]{1,0:T(8,128)S(1)}, u32[]{:S(2)}, u32[]{:S(2)}) collective-permute-start(f32[72,256]{1,0:T(8,128)S(1)} %join.1.own_ref), channel_id=1, source_target_pairs={{0,4},{1,5},{2,6},{3,7},{4,0},{5,1},{6,2},{7,3},{8,12},{9,13},{10,... | collective-permute-start | bytes 221192 | tf_op jit(solution)/shard_map/ppermute | solution.py:488
  17.0 0.9 %copy-done.3 = s32[8,32,128]{2,1,0:T(8,128)S(1)} copy-done((s32[8,32,128]{2,1,0:T(8,128)S(1)}, s32[8,32,128]{2,1,0:T(8,128)}, u32[]{:S(2)}) %copy-start.3) | copy-done | bytes 131096
  17.9 0.9 %copy-done.5 = f32[8,32,128]{2,1,0:T(8,128)S(1)} copy-done((f32[8,32,128]{2,1,0:T(8,128)S(1)}, f32[8,32,128]{2,1,0:T(8,128)}, u32[]{:S(2)}) %copy-start.5) | copy-done | bytes 131096
  18.8 1.4 %own.1 = (f32[4608,128]{1,0:T(8,128)S(1)}, f32[1536,128]{1,0:T(8,128)S(1)}, f32[1536,128]{1,0:T(8,128)S(1)}, f32[9216,128]{1,0:T(8,128)S(1)}, f32[1536,128]{1,0:...) custom-call(s32[8,32,128]{2,1,0:T(8,128)S(1)} %copy-done.3, ...), custom_call_target="tpu_custom_call" | custom-call | tf_op jit(solution)/shard_map/own/pallas_call | solution.py:493
  20.2 0.0 collective-permute-done.5.cb_ref
  20.2 0.0 collective-permute-done.4.ca_ref
  20.2 0.0 collective-permute-done.xa_ref
  20.2 0.0 collective-permute-done.1.xb_ref
  20.2 0.0 copy-start.1
  20.2 1.0 %copy-done.1 = f32[3,8,32,128]{3,2,1,0:T(8,128)S(1)} copy-done((f32[3,8,32,128]{3,2,1,0:T(8,128)S(1)}, f32[3,8,32,128]{3,2,1,0:T(8,128)}, u32[]{:S(2)}) %copy-start.1) | copy-done | bytes 393240
  21.2 7.4 %sweeps.1 = (f32[4608,128]{1,0:T(8,128)S(1)}, f32[1536,128]{1,0:T(8,128)S(1)}, f32[1536,128]{1,0:T(8,128)S(1)}, f32[9216,128]{1,0:T(8,128)S(1)}, f32[1536,128]{1...) custom-call(s32[8,32,128]{2,1,0:T(8,128)S(1)} %copy-done.3, ...), custom_call_target="tpu_custom_call", output_to_operand_aliasing={{0}: (9, {}), {1}: (10, {}), {2}: (11, {}), {3}: (12, {}), ... | custom-call | tf_op jit(solution)/shard_map/sweeps/pallas_call | solution.py:504
  (6 shorter events, 0.0 us)
Async XLA Ops:
  0.6 1.0 %copy-start = (f32[3,8,32,128]{3,2,1,0:T(8,128)S(1)}, f32[3,8,32,128]{3,2,1,0:T(8,128)}, u32[]{:S(2)}) copy-start(f32[3,8,32,128]{3,2,1,0:T(8,128)} %vc_ref.3) | copy-start | bytes 1179652
  1.6 0.9 %copy-start.2 = (s32[8,32,128]{2,1,0:T(8,128)S(1)}, s32[8,32,128]{2,1,0:T(8,128)}, u32[]{:S(2)}) copy-start(s32[8,32,128]{2,1,0:T(8,128)} %ph_ref.5) | copy-start | bytes 393220
  2.5 0.9 %copy-start.4 = (f32[8,32,128]{2,1,0:T(8,128)S(1)}, f32[8,32,128]{2,1,0:T(8,128)}, u32[]{:S(2)}) copy-start(f32[8,32,128]{2,1,0:T(8,128)} %dv_ref.5) | copy-start | bytes 393220
  3.4 0.9 %copy-start.6 = (f32[8,32,128]{2,1,0:T(8,128)S(1)}, f32[8,32,128]{2,1,0:T(8,128)}, u32[]{:S(2)}) copy-start(f32[8,32,128]{2,1,0:T(8,128)} %p_ref.5) | copy-start | bytes 393220
  4.9 15.3 %collective-permute-start = (f32[26,32,128]{2,1,0:T(8,128)S(1)}, f32[26,32,128]{2,1,0:T(8,128)S(1)}, u32[]{:S(2)}, u32[]{:S(2)}) collective-permute-start(f32[26,32,128]{2,1,0:T(8,128)S(1)} %get-tuple-element.22), channel_id=1, source_target_pairs={{0,4},{1,5},{2,6},{3,7},{4,0},{5,1},{6,2},{7,3},{8,12},{9,13},{10,... | collective-permute-start | bytes 1277960 | tf_op jit(solution)/shard_map/ppermute | solution.py:476
  4.9 15.3 %collective-permute-start.1 = (f32[26,32,128]{2,1,0:T(8,128)S(1)}, f32[26,32,128]{2,1,0:T(8,128)S(1)}, u32[]{:S(2)}, u32[]{:S(2)}) collective-permute-start(f32[26,32,128]{2,1,0:T(8,128)S(1)} %get-tuple-element.23), channel_id=1, source_target_pairs={{0,1},{1,0},{2,3},{3,2},{4,8},{5,9},{6,10},{7,11},{8,4},{9,5},{10,... | collective-permute-start | bytes 1277960 | tf_op jit(solution)/shard_map/ppermute | solution.py:475
  7.6 3.4 %collective-permute-start.2 = (f32[32,256]{1,0:T(8,128)S(1)}, f32[32,256]{1,0:T(8,128)S(1)}, u32[]{:S(2)}, u32[]{:S(2)}) collective-permute-start(f32[32,256]{1,0:T(8,128)S(1)} %get-tuple-element.24), channel_id=1, source_target_pairs={{0,1},{4,5},{8,9},{12,13},{16,17},{20,21},{24,25},{28,29},{1,0},{5... | collective-permute-start | bytes 98312 | tf_op jit(solution)/shard_map/ppermute | solution.py:477
  8.9 2.1 %collective-permute-start.3 = (f32[32,256]{1,0:T(8,128)S(1)}, f32[32,256]{1,0:T(8,128)S(1)}, u32[]{:S(2)}, u32[]{:S(2)}) collective-permute-start(f32[32,256]{1,0:T(8,128)S(1)} %get-tuple-element.25), channel_id=1, source_target_pairs={{0,4},{4,0},{8,12},{12,8},{16,20},{20,16},{24,28},{28,24},{1,2},{5... | collective-permute-start | bytes 98312 | tf_op jit(solution)/shard_map/ppermute | solution.py:478
  11.0 9.2 %collective-permute-start.5 = (f32[72,256]{1,0:T(8,128)S(1)}, f32[72,256]{1,0:T(8,128)S(1)}, u32[]{:S(2)}, u32[]{:S(2)}) collective-permute-start(f32[72,256]{1,0:T(8,128)S(1)} %join.1.own_ref), channel_id=1, source_target_pairs={{0,1},{1,0},{2,3},{3,2},{4,8},{5,9},{6,10},{7,11},{8,4},{9,5},{10,... | collective-permute-start | bytes 221192 | tf_op jit(solution)/shard_map/ppermute | solution.py:487
  11.7 8.5 %collective-permute-start.4 = (f32[72,256]{1,0:T(8,128)S(1)}, f32[72,256]{1,0:T(8,128)S(1)}, u32[]{:S(2)}, u32[]{:S(2)}) collective-permute-start(f32[72,256]{1,0:T(8,128)S(1)} %join.1.own_ref), channel_id=1, source_target_pairs={{0,4},{1,5},{2,6},{3,7},{4,0},{5,1},{6,2},{7,3},{8,12},{9,13},{10,... | collective-permute-start | bytes 221192 | tf_op jit(solution)/shard_map/ppermute | solution.py:488
  17.0 0.9 %copy-start.3 = (s32[8,32,128]{2,1,0:T(8,128)S(1)}, s32[8,32,128]{2,1,0:T(8,128)}, u32[]{:S(2)}) copy-start(s32[8,32,128]{2,1,0:T(8,128)} %ph_ref.5) | copy-start | bytes 393220
  17.9 0.9 %copy-start.5 = (f32[8,32,128]{2,1,0:T(8,128)S(1)}, f32[8,32,128]{2,1,0:T(8,128)}, u32[]{:S(2)}) copy-start(f32[8,32,128]{2,1,0:T(8,128)} %dv_ref.5) | copy-start | bytes 393220
  20.2 1.0 %copy-start.1 = (f32[3,8,32,128]{3,2,1,0:T(8,128)S(1)}, f32[3,8,32,128]{3,2,1,0:T(8,128)}, u32[]{:S(2)}) copy-start(f32[3,8,32,128]{3,2,1,0:T(8,128)} %vc_ref.3) | copy-start | bytes 1179652
